TPU v7x, 512 devices: a whole 4x8x8 slice. The times are simulated.
512 devices in a mesh: tm: 8 (over y_hi, core), space: 64 (over y_lo, z, x).
Axes of the slice: x: 4, y: 8 (y_hi: 4, y_lo: 2; y = y_hi * 2 + y_lo), z: 8, core: 2. Of those that a mesh axis runs over, the one named last changes fastest.
Arguments:
- start_states: float32 [8, 3, 512, 4096], P('tm', None, 'space'), may hold values from -6 to 6
- coarse_gain: float32 [3, 512, 4096], P(None, 'space'), may hold values from 0.55 to 0.95
- depth_level: int32 [512, 4096], P('space'), may hold values from 0 to 63
- depth_table: float32 [64], replicated, may hold values from 0.2 to 1
- wet: int32 [512, 4096], P('space'), may hold values 0 or 1
- block_count: int32 [64], P('space'), may hold values from 1 to 8, 320 in all
- neighbour: int32 [512, 4], P('space'), may hold values from -1 to 7
- coriolis: float32 [512, 4096], P('space'), may hold values from -0.5 to 0.5
- tide: float32 [2, 512, 4096], P(None, 'space'), may hold values from -2 to 2
Outputs:
- new_states: float32 [8, 3, 512, 4096], P('tm', None, 'space')
Inputs may be any that keep to these rules, and one draw needn't show every extreme that they name: `block_count`: each column's count is the number of its first slots that hold ocean blocks; some column holds 8. `neighbour`: entries 0 and 1 name slots of the same column, entries 2 and 3 slots of the next and the previous column along the periodic longitude; -1 is a closed face.
All inputs are finite; a program needn't handle non-finite values. No bound on the sum of `wet` on one device may be relied on, other than what follows from the above.
Results may differ from a plain program's by a relative error of at most 0.00007.
Values sent between devices are 32-bit elements; how exact they have to be, the bound alone decides.
A program may use at most 64 MiB of HBM per device.

v0:
```python
import math

import jax
import jax.numpy as jnp
from jax import lax
from jax.sharding import PartitionSpec as P

BS = 64
STEPS = 6
LEVELS = 64


def padded(block, sides, width):
    for axis, dim in sides:
        count = lax.axis_size(axis)
        forward = [(i, i + 1) for i in range(count - 1)]
        forward.append((count - 1, 0))
        backward = [(target, source) for source, target in forward]
        low = lax.ppermute(
            lax.slice_in_dim(block, block.shape[dim] - width, None, axis=dim), axis, forward
        )
        high = lax.ppermute(lax.slice_in_dim(block, 0, width, axis=dim), axis, backward)
        block = jnp.concatenate([low, block, high], axis=dim)
    return block


def passed_along(shard, axis, by):
    size = lax.axis_size(axis)
    return lax.ppermute(shard, axis, [(i, (i + by) % size) for i in range(size)])


def take_edges(edges, index):
    select = (index[:, None] == jnp.arange(edges.shape[0])[None, :]).astype(edges.dtype)
    return jnp.dot(
        select, edges, precision=lax.Precision.HIGHEST, preferred_element_type=jnp.float32
    )


def across(field, west_ghost, east_ghost):
    column = jnp.arange(field.shape[-1]) % BS
    zero = jnp.zeros(field.shape[:-1] + (1,), field.dtype)
    east = jnp.where(
        column == BS - 1,
        jnp.repeat(east_ghost, BS, axis=-1),
        jnp.concatenate([field[:, 1:], zero], -1),
    )
    west = jnp.where(
        column == 0, jnp.repeat(west_ghost, BS, axis=-1), jnp.concatenate([zero, field[:, :-1]], -1)
    )
    return 0.5 * (east - west)


def along(field, north_ghost, south_ghost):
    north = jnp.concatenate([field[:, BS:], north_ghost], -1)
    south = jnp.concatenate([south_ghost, field[:, :-BS]], -1)
    return 0.5 * (north - south)


def edge_pair(field):
    return jnp.stack([field[:, 0::BS], field[:, BS - 1 :: BS]])


def body(
    start_states, coarse_gain, depth_level, depth_table, wet, block_count, neighbour, coriolis, tide
):
    slots_here = wet.shape[0]
    slot = jnp.arange(slots_here)
    live = wet.astype(jnp.float32) * (slot < block_count[0]).astype(jnp.float32)[:, None]
    level_ids = jnp.arange(LEVELS)[:, None]

    def depth_row(levels):
        return jnp.sum(
            jnp.where(levels[None, :] == level_ids, depth_table[:, None], jnp.float32(0.0)), axis=0
        )

    depth = lax.map(depth_row, depth_level)
    north_id = neighbour[:, 0]
    south_id = neighbour[:, 1]
    east_id = neighbour[:, 2]
    west_id = neighbour[:, 3]
    start = start_states * live
    slices = lax.axis_size("tm")
    omega = 2.0 * math.pi / (slices * STEPS)
    first_time = lax.axis_index("tm").astype(jnp.float32) * STEPS
    level, east_vel, north_vel = (start[0, 0], start[0, 1], start[0, 2])
    for step in range(STEPS):
        angle = (first_time + step) * omega
        source = tide[0] * jnp.cos(angle) + tide[1] * jnp.sin(angle)
        flux_x = depth * east_vel
        flux_y = depth * north_vel
        bordered = padded(edge_pair(flux_x), (("space", 0),), 1)
        div = across(flux_x, take_edges(bordered[0], west_id), take_edges(bordered[3], east_id))
        div = div + along(
            flux_y, take_edges(flux_y[:, :BS], north_id), take_edges(flux_y[:, -BS:], south_id)
        )
        level = (level + 0.3 * (source - div)) * live
        bordered = padded(edge_pair(level), (("space", 0),), 1)
        slope_x = across(level, take_edges(bordered[0], west_id), take_edges(bordered[3], east_id))
        slope_y = along(
            level, take_edges(level[:, :BS], north_id), take_edges(level[:, -BS:], south_id)
        )
        new_east = (east_vel + 0.3 * (coriolis * north_vel - slope_x - 0.05 * east_vel)) * live
        north_vel = (north_vel + 0.3 * (-coriolis * east_vel - slope_y - 0.05 * north_vel)) * live
        east_vel = new_east
    fine = jnp.stack([level, east_vel, north_vel])[None]
    defect = fine - coarse_gain * start

    def advance(turn, partial_sum):
        return defect + coarse_gain * passed_along(partial_sum, "tm", 1)

    partial_sum = lax.fori_loop(0, slices - 1, advance, defect)
    total = passed_along(partial_sum, "tm", 1)
    return total / (1.0 - coarse_gain**slices)


def solution(mesh):
    return jax.shard_map(
        body,
        mesh=mesh,
        in_specs=(
            P("tm", None, "space", None),
            P(None, "space", None),
            P("space", None),
            P(),
            P("space", None),
            P("space"),
            P("space", None),
            P("space", None),
            P(None, "space", None),
        ),
        out_specs=P("tm", None, "space", None),
        check_vma=False,
    )
```

profile of v0, /device:TPU:1, one launch (start us, length us, event | category | flops | bytes accessed | tf_op | source)
XLA Modules:
  0.0 293.1 jit_solution(8180846715036717408)
XLA Ops:
  1.3 12.6 %while.22 = (s32[]{:T(128)}, f32[8,4096]{1,0:T(8,128)S(1)}, s32[8,4096]{1,0:T(8,128)}, f32[64]{0:T(128)S(1)}, s32[]{:T(128)}, /*index=5*/s32[]{:T(128)}) while((s32[]{:T(128)}, f32[8,4096]{1,0:T(8,128)S(1)}, s32[8,4096]{1,0:T(8,128)}, f32[64]{0:T(128)S(1)}, s32[]{:T(128)}, /*index=5*/s32[]{:T(128)}) %tuple.91), condition=%wide.region_2.3_spmd.clone, body=%wide.region_0.2_spmd.clone.sunk | while | flops 782338 | bytes 98637 | solution.py:76
  15.2 14.7 %collective-permute-start.1 = (f32[1,8,64]{2,1,0:T(8,128)S(1)}, f32[1,8,64]{2,1,0:T(8,128)S(1)}, u32[]{:S(2)}, u32[]{:S(2)}) collective-permute-start(f32[1,8,64]{2,1,0:T(8,128)S(1)} %bitcast.175), channel_id=1, source_target_pairs={{1,0},{2,1},{3,2},{4,3},{5,4},{6,5},{7,6},{8,7},{9,8},{10,9},{11,1... | collective-permute-start | bytes 6152 | tf_op jit(solution)/shard_map/ppermute | solution.py:22
  34.1 4.6 %collective-permute-done.2 = f32[1,8,64]{2,1,0:T(8,128)S(1)} collective-permute-done((f32[1,8,64]{2,1,0:T(8,128)S(1)}, f32[1,8,64]{2,1,0:T(8,128)S(1)}, u32[]{:S(2)}, u32[]{:S(2)}) %collective-permute-start.2) | collective-permute-done | bytes 2080 | tf_op jit(solution)/shard_map/ppermute | solution.py:19
  46.7 5.8 %collective-permute-done.4 = f32[1,8,64]{2,1,0:T(8,128)S(1)} collective-permute-done((f32[1,8,64]{2,1,0:T(8,128)S(1)}, f32[1,8,64]{2,1,0:T(8,128)S(1)}, u32[]{:S(2)}, u32[]{:S(2)}) %collective-permute-start.4) | collective-permute-done | bytes 2080 | tf_op jit(solution)/shard_map/ppermute | solution.py:19
  60.6 4.7 %collective-permute-done.6 = f32[1,8,64]{2,1,0:T(8,128)S(1)} collective-permute-done((f32[1,8,64]{2,1,0:T(8,128)S(1)}, f32[1,8,64]{2,1,0:T(8,128)S(1)}, u32[]{:S(2)}, u32[]{:S(2)}) %collective-permute-start.6) | collective-permute-done | bytes 2080 | tf_op jit(solution)/shard_map/ppermute | solution.py:19
  72.6 4.7 %collective-permute-done.8 = f32[1,8,64]{2,1,0:T(8,128)S(1)} collective-permute-done((f32[1,8,64]{2,1,0:T(8,128)S(1)}, f32[1,8,64]{2,1,0:T(8,128)S(1)}, u32[]{:S(2)}, u32[]{:S(2)}) %collective-permute-start.8) | collective-permute-done | bytes 2080 | tf_op jit(solution)/shard_map/ppermute | solution.py:19
  84.6 4.7 %collective-permute-done.10 = f32[1,8,64]{2,1,0:T(8,128)S(1)} collective-permute-done((f32[1,8,64]{2,1,0:T(8,128)S(1)}, f32[1,8,64]{2,1,0:T(8,128)S(1)}, u32[]{:S(2)}, u32[]{:S(2)}) %collective-permute-start.10) | collective-permute-done | bytes 2080 | tf_op jit(solution)/shard_map/ppermute | solution.py:19
  92.7 3.4 %collective-permute-start.12 = (f32[1,8,64]{2,1,0:T(8,128)S(1)}, f32[1,8,64]{2,1,0:T(8,128)S(1)}, u32[]{:S(2)}, u32[]{:S(2)}) collective-permute-start(f32[1,8,64]{2,1,0:T(8,128)S(1)} %bitcast.195), channel_id=1, source_target_pairs={{0,1},{1,2},{2,3},{3,4},{4,5},{5,6},{6,7},{7,8},{8,9},{9,10},{10,1... | collective-permute-start | bytes 6152 | tf_op jit(solution)/shard_map/ppermute | solution.py:19
  96.6 4.7 %collective-permute-done.12 = f32[1,8,64]{2,1,0:T(8,128)S(1)} collective-permute-done((f32[1,8,64]{2,1,0:T(8,128)S(1)}, f32[1,8,64]{2,1,0:T(8,128)S(1)}, u32[]{:S(2)}, u32[]{:S(2)}) %collective-permute-start.12) | collective-permute-done | bytes 2080 | tf_op jit(solution)/shard_map/ppermute | solution.py:19
  108.6 4.7 %collective-permute-done.14 = f32[1,8,64]{2,1,0:T(8,128)S(1)} collective-permute-done((f32[1,8,64]{2,1,0:T(8,128)S(1)}, f32[1,8,64]{2,1,0:T(8,128)S(1)}, u32[]{:S(2)}, u32[]{:S(2)}) %collective-permute-start.14) | collective-permute-done | bytes 2080 | tf_op jit(solution)/shard_map/ppermute | solution.py:19
  120.6 4.7 %collective-permute-done.16 = f32[1,8,64]{2,1,0:T(8,128)S(1)} collective-permute-done((f32[1,8,64]{2,1,0:T(8,128)S(1)}, f32[1,8,64]{2,1,0:T(8,128)S(1)}, u32[]{:S(2)}, u32[]{:S(2)}) %collective-permute-start.16) | collective-permute-done | bytes 2080 | tf_op jit(solution)/shard_map/ppermute | solution.py:19
  132.6 4.7 %collective-permute-done.18 = f32[1,8,64]{2,1,0:T(8,128)S(1)} collective-permute-done((f32[1,8,64]{2,1,0:T(8,128)S(1)}, f32[1,8,64]{2,1,0:T(8,128)S(1)}, u32[]{:S(2)}, u32[]{:S(2)}) %collective-permute-start.18) | collective-permute-done | bytes 2080 | tf_op jit(solution)/shard_map/ppermute | solution.py:19
  144.6 4.7 %collective-permute-done.20 = f32[1,8,64]{2,1,0:T(8,128)S(1)} collective-permute-done((f32[1,8,64]{2,1,0:T(8,128)S(1)}, f32[1,8,64]{2,1,0:T(8,128)S(1)}, u32[]{:S(2)}, u32[]{:S(2)}) %collective-permute-start.20) | collective-permute-done | bytes 2080 | tf_op jit(solution)/shard_map/ppermute | solution.py:19
  156.6 4.7 %collective-permute-done.22 = f32[1,8,64]{2,1,0:T(8,128)S(1)} collective-permute-done((f32[1,8,64]{2,1,0:T(8,128)S(1)}, f32[1,8,64]{2,1,0:T(8,128)S(1)}, u32[]{:S(2)}, u32[]{:S(2)}) %collective-permute-start.22) | collective-permute-done | bytes 2080 | tf_op jit(solution)/shard_map/ppermute | solution.py:19
  168.6 4.7 %collective-permute-done.24 = f32[1,8,64]{2,1,0:T(8,128)S(1)} collective-permute-done((f32[1,8,64]{2,1,0:T(8,128)S(1)}, f32[1,8,64]{2,1,0:T(8,128)S(1)}, u32[]{:S(2)}, u32[]{:S(2)}) %collective-permute-start.24) | collective-permute-done | bytes 2080 | tf_op jit(solution)/shard_map/ppermute | solution.py:19
  175.0 104.3 %while.21 = (s32[]{:T(128)}, f32[1,3,8,4096]{3,2,1,0:T(8,128)S(1)}, f32[3,8,4096]{2,1,0:T(8,128)S(1)}, f32[1,3,8,4096]{3,2,1,0:T(8,128)S(1)}, s32[]{:T(128)}) while((s32[]{:T(128)}, f32[1,3,8,4096]{3,2,1,0:T(8,128)S(1)}, f32[3,8,4096]{2,1,0:T(8,128)S(1)}, f32[1,3,8,4096]{3,2,1,0:T(8,128)S(1)}, s32[]{:T(128)}) %tuple.90), condition=%wide.region_4.5_spmd, body=%wide.region_3.4_spmd.sunk | while | flops 196610 | bytes 3145829 | solution.py:111
  175.0 18.3 %collective-permute-start = (f32[1,3,8,4096]{3,2,1,0:T(8,128)S(1)}, f32[1,3,8,4096]{3,2,1,0:T(8,128)S(1)}, u32[]{:S(2)}, u32[]{:S(2)}) collective-permute-start(f32[1,3,8,4096]{3,2,1,0:T(8,128)S(1)} %get-tuple-element.244), channel_id=1, source_target_pairs={{0,64},{64,128},{128,192},{192,256},{256,320},{320,384},{384,448},... | collective-permute-start | bytes 1179656 | tf_op jit(solution)/shard_map/while/body/eval_jaxpr/ppermute | solution.py:29
  193.3 6.0 %collective-permute-done = f32[1,3,8,4096]{3,2,1,0:T(8,128)S(1)} collective-permute-done((f32[1,3,8,4096]{3,2,1,0:T(8,128)S(1)}, f32[1,3,8,4096]{3,2,1,0:T(8,128)S(1)}, u32[]{:S(2)}, u32[]{:S(2)}) %collective-permute-start) | collective-permute-done | bytes 393248 | tf_op jit(solution)/shard_map/while/body/eval_jaxpr/ppermute | solution.py:29
  199.3 8.2 %collective-permute-start = (f32[1,3,8,4096]{3,2,1,0:T(8,128)S(1)}, f32[1,3,8,4096]{3,2,1,0:T(8,128)S(1)}, u32[]{:S(2)}, u32[]{:S(2)}) collective-permute-start(f32[1,3,8,4096]{3,2,1,0:T(8,128)S(1)} %get-tuple-element.244), channel_id=1, source_target_pairs={{0,64},{64,128},{128,192},{192,256},{256,320},{320,384},{384,448},... | collective-permute-start | bytes 1179656 | tf_op jit(solution)/shard_map/while/body/eval_jaxpr/ppermute | solution.py:29
  207.6 9.0 %collective-permute-done = f32[1,3,8,4096]{3,2,1,0:T(8,128)S(1)} collective-permute-done((f32[1,3,8,4096]{3,2,1,0:T(8,128)S(1)}, f32[1,3,8,4096]{3,2,1,0:T(8,128)S(1)}, u32[]{:S(2)}, u32[]{:S(2)}) %collective-permute-start) | collective-permute-done | bytes 393248 | tf_op jit(solution)/shard_map/while/body/eval_jaxpr/ppermute | solution.py:29
  216.6 5.3 %collective-permute-start = (f32[1,3,8,4096]{3,2,1,0:T(8,128)S(1)}, f32[1,3,8,4096]{3,2,1,0:T(8,128)S(1)}, u32[]{:S(2)}, u32[]{:S(2)}) collective-permute-start(f32[1,3,8,4096]{3,2,1,0:T(8,128)S(1)} %get-tuple-element.244), channel_id=1, source_target_pairs={{0,64},{64,128},{128,192},{192,256},{256,320},{320,384},{384,448},... | collective-permute-start | bytes 1179656 | tf_op jit(solution)/shard_map/while/body/eval_jaxpr/ppermute | solution.py:29
  221.9 8.5 %collective-permute-done = f32[1,3,8,4096]{3,2,1,0:T(8,128)S(1)} collective-permute-done((f32[1,3,8,4096]{3,2,1,0:T(8,128)S(1)}, f32[1,3,8,4096]{3,2,1,0:T(8,128)S(1)}, u32[]{:S(2)}, u32[]{:S(2)}) %collective-permute-start) | collective-permute-done | bytes 393248 | tf_op jit(solution)/shard_map/while/body/eval_jaxpr/ppermute | solution.py:29
  230.4 5.3 %collective-permute-start = (f32[1,3,8,4096]{3,2,1,0:T(8,128)S(1)}, f32[1,3,8,4096]{3,2,1,0:T(8,128)S(1)}, u32[]{:S(2)}, u32[]{:S(2)}) collective-permute-start(f32[1,3,8,4096]{3,2,1,0:T(8,128)S(1)} %get-tuple-element.244), channel_id=1, source_target_pairs={{0,64},{64,128},{128,192},{192,256},{256,320},{320,384},{384,448},... | collective-permute-start | bytes 1179656 | tf_op jit(solution)/shard_map/while/body/eval_jaxpr/ppermute | solution.py:29
  235.8 6.0 %collective-permute-done = f32[1,3,8,4096]{3,2,1,0:T(8,128)S(1)} collective-permute-done((f32[1,3,8,4096]{3,2,1,0:T(8,128)S(1)}, f32[1,3,8,4096]{3,2,1,0:T(8,128)S(1)}, u32[]{:S(2)}, u32[]{:S(2)}) %collective-permute-start) | collective-permute-done | bytes 393248 | tf_op jit(solution)/shard_map/while/body/eval_jaxpr/ppermute | solution.py:29
  241.9 5.4 %collective-permute-start = (f32[1,3,8,4096]{3,2,1,0:T(8,128)S(1)}, f32[1,3,8,4096]{3,2,1,0:T(8,128)S(1)}, u32[]{:S(2)}, u32[]{:S(2)}) collective-permute-start(f32[1,3,8,4096]{3,2,1,0:T(8,128)S(1)} %get-tuple-element.244), channel_id=1, source_target_pairs={{0,64},{64,128},{128,192},{192,256},{256,320},{320,384},{384,448},... | collective-permute-start | bytes 1179656 | tf_op jit(solution)/shard_map/while/body/eval_jaxpr/ppermute | solution.py:29
  247.3 5.9 %collective-permute-done = f32[1,3,8,4096]{3,2,1,0:T(8,128)S(1)} collective-permute-done((f32[1,3,8,4096]{3,2,1,0:T(8,128)S(1)}, f32[1,3,8,4096]{3,2,1,0:T(8,128)S(1)}, u32[]{:S(2)}, u32[]{:S(2)}) %collective-permute-start) | collective-permute-done | bytes 393248 | tf_op jit(solution)/shard_map/while/body/eval_jaxpr/ppermute | solution.py:29
  253.3 5.4 %collective-permute-start = (f32[1,3,8,4096]{3,2,1,0:T(8,128)S(1)}, f32[1,3,8,4096]{3,2,1,0:T(8,128)S(1)}, u32[]{:S(2)}, u32[]{:S(2)}) collective-permute-start(f32[1,3,8,4096]{3,2,1,0:T(8,128)S(1)} %get-tuple-element.244), channel_id=1, source_target_pairs={{0,64},{64,128},{128,192},{192,256},{256,320},{320,384},{384,448},... | collective-permute-start | bytes 1179656 | tf_op jit(solution)/shard_map/while/body/eval_jaxpr/ppermute | solution.py:29
  258.7 6.2 %collective-permute-done = f32[1,3,8,4096]{3,2,1,0:T(8,128)S(1)} collective-permute-done((f32[1,3,8,4096]{3,2,1,0:T(8,128)S(1)}, f32[1,3,8,4096]{3,2,1,0:T(8,128)S(1)}, u32[]{:S(2)}, u32[]{:S(2)}) %collective-permute-start) | collective-permute-done | bytes 393248 | tf_op jit(solution)/shard_map/while/body/eval_jaxpr/ppermute | solution.py:29
  265.0 5.4 %collective-permute-start = (f32[1,3,8,4096]{3,2,1,0:T(8,128)S(1)}, f32[1,3,8,4096]{3,2,1,0:T(8,128)S(1)}, u32[]{:S(2)}, u32[]{:S(2)}) collective-permute-start(f32[1,3,8,4096]{3,2,1,0:T(8,128)S(1)} %get-tuple-element.244), channel_id=1, source_target_pairs={{0,64},{64,128},{128,192},{192,256},{256,320},{320,384},{384,448},... | collective-permute-start | bytes 1179656 | tf_op jit(solution)/shard_map/while/body/eval_jaxpr/ppermute | solution.py:29
  270.4 8.9 %collective-permute-done = f32[1,3,8,4096]{3,2,1,0:T(8,128)S(1)} collective-permute-done((f32[1,3,8,4096]{3,2,1,0:T(8,128)S(1)}, f32[1,3,8,4096]{3,2,1,0:T(8,128)S(1)}, u32[]{:S(2)}, u32[]{:S(2)}) %collective-permute-start) | collective-permute-done | bytes 393248 | tf_op jit(solution)/shard_map/while/body/eval_jaxpr/ppermute | solution.py:29
  279.3 5.3 %collective-permute-start.25 = (f32[1,3,8,4096]{3,2,1,0:T(8,128)S(1)}, f32[1,3,8,4096]{3,2,1,0:T(8,128)S(1)}, u32[]{:S(2)}, u32[]{:S(2)}) collective-permute-start(f32[1,3,8,4096]{3,2,1,0:T(8,128)S(1)} %get-tuple-element.55), channel_id=1, source_target_pairs={{0,64},{64,128},{128,192},{192,256},{256,320},{320,384},{384,448},... | collective-permute-start | bytes 1179656 | tf_op jit(solution)/shard_map/ppermute | solution.py:29
  284.6 7.7 %collective-permute-done.25 = f32[1,3,8,4096]{3,2,1,0:T(8,128)S(1)} collective-permute-done((f32[1,3,8,4096]{3,2,1,0:T(8,128)S(1)}, f32[1,3,8,4096]{3,2,1,0:T(8,128)S(1)}, u32[]{:S(2)}, u32[]{:S(2)}) %collective-permute-start.25) | collective-permute-done | bytes 393248 | tf_op jit(solution)/shard_map/ppermute | solution.py:29
  (245 shorter events, 97.5 us)
Async XLA Ops:
  15.2 18.4 %collective-permute-start.1 = (f32[1,8,64]{2,1,0:T(8,128)S(1)}, f32[1,8,64]{2,1,0:T(8,128)S(1)}, u32[]{:S(2)}, u32[]{:S(2)}) collective-permute-start(f32[1,8,64]{2,1,0:T(8,128)S(1)} %bitcast.175), channel_id=1, source_target_pairs={{1,0},{2,1},{3,2},{4,3},{5,4},{6,5},{7,6},{8,7},{9,8},{10,9},{11,1... | collective-permute-start | bytes 6152 | tf_op jit(solution)/shard_map/ppermute | solution.py:22
  30.1 8.6 %collective-permute-start.2 = (f32[1,8,64]{2,1,0:T(8,128)S(1)}, f32[1,8,64]{2,1,0:T(8,128)S(1)}, u32[]{:S(2)}, u32[]{:S(2)}) collective-permute-start(f32[1,8,64]{2,1,0:T(8,128)S(1)} %bitcast.174), channel_id=1, source_target_pairs={{0,1},{1,2},{2,3},{3,4},{4,5},{5,6},{6,7},{7,8},{8,9},{9,10},{10,1... | collective-permute-start | bytes 6152 | tf_op jit(solution)/shard_map/ppermute | solution.py:19
  40.7 5.6 %collective-permute-start.3 = (f32[1,8,64]{2,1,0:T(8,128)S(1)}, f32[1,8,64]{2,1,0:T(8,128)S(1)}, u32[]{:S(2)}, u32[]{:S(2)}) collective-permute-start(f32[1,8,64]{2,1,0:T(8,128)S(1)} %bitcast.182), channel_id=1, source_target_pairs={{1,0},{2,1},{3,2},{4,3},{5,4},{6,5},{7,6},{8,7},{9,8},{10,9},{11,1... | collective-permute-start | bytes 6152 | tf_op jit(solution)/shard_map/ppermute | solution.py:22
  44.0 8.6 %collective-permute-start.4 = (f32[1,8,64]{2,1,0:T(8,128)S(1)}, f32[1,8,64]{2,1,0:T(8,128)S(1)}, u32[]{:S(2)}, u32[]{:S(2)}) collective-permute-start(f32[1,8,64]{2,1,0:T(8,128)S(1)} %bitcast.193), channel_id=1, source_target_pairs={{0,1},{1,2},{2,3},{3,4},{4,5},{5,6},{6,7},{7,8},{8,9},{9,10},{10,1... | collective-permute-start | bytes 6152 | tf_op jit(solution)/shard_map/ppermute | solution.py:19
  54.5 5.6 %collective-permute-start.5 = (f32[1,8,64]{2,1,0:T(8,128)S(1)}, f32[1,8,64]{2,1,0:T(8,128)S(1)}, u32[]{:S(2)}, u32[]{:S(2)}) collective-permute-start(f32[1,8,64]{2,1,0:T(8,128)S(1)} %bitcast.176), channel_id=1, source_target_pairs={{1,0},{2,1},{3,2},{4,3},{5,4},{6,5},{7,6},{8,7},{9,8},{10,9},{11,1... | collective-permute-start | bytes 6152 | tf_op jit(solution)/shard_map/ppermute | solution.py:22
  56.8 8.6 %collective-permute-start.6 = (f32[1,8,64]{2,1,0:T(8,128)S(1)}, f32[1,8,64]{2,1,0:T(8,128)S(1)}, u32[]{:S(2)}, u32[]{:S(2)}) collective-permute-start(f32[1,8,64]{2,1,0:T(8,128)S(1)} %bitcast.187), channel_id=1, source_target_pairs={{0,1},{1,2},{2,3},{3,4},{4,5},{5,6},{6,7},{7,8},{8,9},{9,10},{10,1... | collective-permute-start | bytes 6152 | tf_op jit(solution)/shard_map/ppermute | solution.py:19
  66.5 5.6 %collective-permute-start.7 = (f32[1,8,64]{2,1,0:T(8,128)S(1)}, f32[1,8,64]{2,1,0:T(8,128)S(1)}, u32[]{:S(2)}, u32[]{:S(2)}) collective-permute-start(f32[1,8,64]{2,1,0:T(8,128)S(1)} %bitcast.183), channel_id=1, source_target_pairs={{1,0},{2,1},{3,2},{4,3},{5,4},{6,5},{7,6},{8,7},{9,8},{10,9},{11,1... | collective-permute-start | bytes 6152 | tf_op jit(solution)/shard_map/ppermute | solution.py:22
  68.7 8.6 %collective-permute-start.8 = (f32[1,8,64]{2,1,0:T(8,128)S(1)}, f32[1,8,64]{2,1,0:T(8,128)S(1)}, u32[]{:S(2)}, u32[]{:S(2)}) collective-permute-start(f32[1,8,64]{2,1,0:T(8,128)S(1)} %bitcast.194), channel_id=1, source_target_pairs={{0,1},{1,2},{2,3},{3,4},{4,5},{5,6},{6,7},{7,8},{8,9},{9,10},{10,1... | collective-permute-start | bytes 6152 | tf_op jit(solution)/shard_map/ppermute | solution.py:19
  78.5 5.6 %collective-permute-start.9 = (f32[1,8,64]{2,1,0:T(8,128)S(1)}, f32[1,8,64]{2,1,0:T(8,128)S(1)}, u32[]{:S(2)}, u32[]{:S(2)}) collective-permute-start(f32[1,8,64]{2,1,0:T(8,128)S(1)} %bitcast.177), channel_id=1, source_target_pairs={{1,0},{2,1},{3,2},{4,3},{5,4},{6,5},{7,6},{8,7},{9,8},{10,9},{11,1... | collective-permute-start | bytes 6152 | tf_op jit(solution)/shard_map/ppermute | solution.py:22
  80.8 8.6 %collective-permute-start.10 = (f32[1,8,64]{2,1,0:T(8,128)S(1)}, f32[1,8,64]{2,1,0:T(8,128)S(1)}, u32[]{:S(2)}, u32[]{:S(2)}) collective-permute-start(f32[1,8,64]{2,1,0:T(8,128)S(1)} %bitcast.188), channel_id=1, source_target_pairs={{0,1},{1,2},{2,3},{3,4},{4,5},{5,6},{6,7},{7,8},{8,9},{9,10},{10,1... | collective-permute-start | bytes 6152 | tf_op jit(solution)/shard_map/ppermute | solution.py:19
  90.5 5.6 %collective-permute-start.11 = (f32[1,8,64]{2,1,0:T(8,128)S(1)}, f32[1,8,64]{2,1,0:T(8,128)S(1)}, u32[]{:S(2)}, u32[]{:S(2)}) collective-permute-start(f32[1,8,64]{2,1,0:T(8,128)S(1)} %bitcast.184), channel_id=1, source_target_pairs={{1,0},{2,1},{3,2},{4,3},{5,4},{6,5},{7,6},{8,7},{9,8},{10,9},{11,1... | collective-permute-start | bytes 6152 | tf_op jit(solution)/shard_map/ppermute | solution.py:22
  92.7 8.6 %collective-permute-start.12 = (f32[1,8,64]{2,1,0:T(8,128)S(1)}, f32[1,8,64]{2,1,0:T(8,128)S(1)}, u32[]{:S(2)}, u32[]{:S(2)}) collective-permute-start(f32[1,8,64]{2,1,0:T(8,128)S(1)} %bitcast.195), channel_id=1, source_target_pairs={{0,1},{1,2},{2,3},{3,4},{4,5},{5,6},{6,7},{7,8},{8,9},{9,10},{10,1... | collective-permute-start | bytes 6152 | tf_op jit(solution)/shard_map/ppermute | solution.py:19
  102.5 5.6 %collective-permute-start.13 = (f32[1,8,64]{2,1,0:T(8,128)S(1)}, f32[1,8,64]{2,1,0:T(8,128)S(1)}, u32[]{:S(2)}, u32[]{:S(2)}) collective-permute-start(f32[1,8,64]{2,1,0:T(8,128)S(1)} %bitcast.178), channel_id=1, source_target_pairs={{1,0},{2,1},{3,2},{4,3},{5,4},{6,5},{7,6},{8,7},{9,8},{10,9},{11,1... | collective-permute-start | bytes 6152 | tf_op jit(solution)/shard_map/ppermute | solution.py:22
  104.8 8.6 %collective-permute-start.14 = (f32[1,8,64]{2,1,0:T(8,128)S(1)}, f32[1,8,64]{2,1,0:T(8,128)S(1)}, u32[]{:S(2)}, u32[]{:S(2)}) collective-permute-start(f32[1,8,64]{2,1,0:T(8,128)S(1)} %bitcast.189), channel_id=1, source_target_pairs={{0,1},{1,2},{2,3},{3,4},{4,5},{5,6},{6,7},{7,8},{8,9},{9,10},{10,1... | collective-permute-start | bytes 6152 | tf_op jit(solution)/shard_map/ppermute | solution.py:19
  114.5 5.6 %collective-permute-start.15 = (f32[1,8,64]{2,1,0:T(8,128)S(1)}, f32[1,8,64]{2,1,0:T(8,128)S(1)}, u32[]{:S(2)}, u32[]{:S(2)}) collective-permute-start(f32[1,8,64]{2,1,0:T(8,128)S(1)} %bitcast.185), channel_id=1, source_target_pairs={{1,0},{2,1},{3,2},{4,3},{5,4},{6,5},{7,6},{8,7},{9,8},{10,9},{11,1... | collective-permute-start | bytes 6152 | tf_op jit(solution)/shard_map/ppermute | solution.py:22
  116.7 8.6 %collective-permute-start.16 = (f32[1,8,64]{2,1,0:T(8,128)S(1)}, f32[1,8,64]{2,1,0:T(8,128)S(1)}, u32[]{:S(2)}, u32[]{:S(2)}) collective-permute-start(f32[1,8,64]{2,1,0:T(8,128)S(1)} %bitcast.196), channel_id=1, source_target_pairs={{0,1},{1,2},{2,3},{3,4},{4,5},{5,6},{6,7},{7,8},{8,9},{9,10},{10,1... | collective-permute-start | bytes 6152 | tf_op jit(solution)/shard_map/ppermute | solution.py:19
  126.5 5.6 %collective-permute-start.17 = (f32[1,8,64]{2,1,0:T(8,128)S(1)}, f32[1,8,64]{2,1,0:T(8,128)S(1)}, u32[]{:S(2)}, u32[]{:S(2)}) collective-permute-start(f32[1,8,64]{2,1,0:T(8,128)S(1)} %bitcast.179), channel_id=1, source_target_pairs={{1,0},{2,1},{3,2},{4,3},{5,4},{6,5},{7,6},{8,7},{9,8},{10,9},{11,1... | collective-permute-start | bytes 6152 | tf_op jit(solution)/shard_map/ppermute | solution.py:22
  128.8 8.6 %collective-permute-start.18 = (f32[1,8,64]{2,1,0:T(8,128)S(1)}, f32[1,8,64]{2,1,0:T(8,128)S(1)}, u32[]{:S(2)}, u32[]{:S(2)}) collective-permute-start(f32[1,8,64]{2,1,0:T(8,128)S(1)} %bitcast.190), channel_id=1, source_target_pairs={{0,1},{1,2},{2,3},{3,4},{4,5},{5,6},{6,7},{7,8},{8,9},{9,10},{10,1... | collective-permute-start | bytes 6152 | tf_op jit(solution)/shard_map/ppermute | solution.py:19
  138.5 5.6 %collective-permute-start.19 = (f32[1,8,64]{2,1,0:T(8,128)S(1)}, f32[1,8,64]{2,1,0:T(8,128)S(1)}, u32[]{:S(2)}, u32[]{:S(2)}) collective-permute-start(f32[1,8,64]{2,1,0:T(8,128)S(1)} %bitcast.186), channel_id=1, source_target_pairs={{1,0},{2,1},{3,2},{4,3},{5,4},{6,5},{7,6},{8,7},{9,8},{10,9},{11,1... | collective-permute-start | bytes 6152 | tf_op jit(solution)/shard_map/ppermute | solution.py:22
  140.7 8.6 %collective-permute-start.20 = (f32[1,8,64]{2,1,0:T(8,128)S(1)}, f32[1,8,64]{2,1,0:T(8,128)S(1)}, u32[]{:S(2)}, u32[]{:S(2)}) collective-permute-start(f32[1,8,64]{2,1,0:T(8,128)S(1)} %bitcast.197), channel_id=1, source_target_pairs={{0,1},{1,2},{2,3},{3,4},{4,5},{5,6},{6,7},{7,8},{8,9},{9,10},{10,1... | collective-permute-start | bytes 6152 | tf_op jit(solution)/shard_map/ppermute | solution.py:19
  150.5 5.6 %collective-permute-start.21 = (f32[1,8,64]{2,1,0:T(8,128)S(1)}, f32[1,8,64]{2,1,0:T(8,128)S(1)}, u32[]{:S(2)}, u32[]{:S(2)}) collective-permute-start(f32[1,8,64]{2,1,0:T(8,128)S(1)} %bitcast.180), channel_id=1, source_target_pairs={{1,0},{2,1},{3,2},{4,3},{5,4},{6,5},{7,6},{8,7},{9,8},{10,9},{11,1... | collective-permute-start | bytes 6152 | tf_op jit(solution)/shard_map/ppermute | solution.py:22
  152.8 8.6 %collective-permute-start.22 = (f32[1,8,64]{2,1,0:T(8,128)S(1)}, f32[1,8,64]{2,1,0:T(8,128)S(1)}, u32[]{:S(2)}, u32[]{:S(2)}) collective-permute-start(f32[1,8,64]{2,1,0:T(8,128)S(1)} %bitcast.191), channel_id=1, source_target_pairs={{0,1},{1,2},{2,3},{3,4},{4,5},{5,6},{6,7},{7,8},{8,9},{9,10},{10,1... | collective-permute-start | bytes 6152 | tf_op jit(solution)/shard_map/ppermute | solution.py:19
  162.5 5.6 %collective-permute-start.23 = (f32[1,8,64]{2,1,0:T(8,128)S(1)}, f32[1,8,64]{2,1,0:T(8,128)S(1)}, u32[]{:S(2)}, u32[]{:S(2)}) collective-permute-start(f32[1,8,64]{2,1,0:T(8,128)S(1)} %bitcast.181), channel_id=1, source_target_pairs={{1,0},{2,1},{3,2},{4,3},{5,4},{6,5},{7,6},{8,7},{9,8},{10,9},{11,1... | collective-permute-start | bytes 6152 | tf_op jit(solution)/shard_map/ppermute | solution.py:22
  164.7 8.6 %collective-permute-start.24 = (f32[1,8,64]{2,1,0:T(8,128)S(1)}, f32[1,8,64]{2,1,0:T(8,128)S(1)}, u32[]{:S(2)}, u32[]{:S(2)}) collective-permute-start(f32[1,8,64]{2,1,0:T(8,128)S(1)} %bitcast.192), channel_id=1, source_target_pairs={{0,1},{1,2},{2,3},{3,4},{4,5},{5,6},{6,7},{7,8},{8,9},{9,10},{10,1... | collective-permute-start | bytes 6152 | tf_op jit(solution)/shard_map/ppermute | solution.py:19
  175.0 24.3 %collective-permute-start = (f32[1,3,8,4096]{3,2,1,0:T(8,128)S(1)}, f32[1,3,8,4096]{3,2,1,0:T(8,128)S(1)}, u32[]{:S(2)}, u32[]{:S(2)}) collective-permute-start(f32[1,3,8,4096]{3,2,1,0:T(8,128)S(1)} %get-tuple-element.244), channel_id=1, source_target_pairs={{0,64},{64,128},{128,192},{192,256},{256,320},{320,384},{384,448},... | collective-permute-start | bytes 1179656 | tf_op jit(solution)/shard_map/while/body/eval_jaxpr/ppermute | solution.py:29
  199.3 17.2 %collective-permute-start = (f32[1,3,8,4096]{3,2,1,0:T(8,128)S(1)}, f32[1,3,8,4096]{3,2,1,0:T(8,128)S(1)}, u32[]{:S(2)}, u32[]{:S(2)}) collective-permute-start(f32[1,3,8,4096]{3,2,1,0:T(8,128)S(1)} %get-tuple-element.244), channel_id=1, source_target_pairs={{0,64},{64,128},{128,192},{192,256},{256,320},{320,384},{384,448},... | collective-permute-start | bytes 1179656 | tf_op jit(solution)/shard_map/while/body/eval_jaxpr/ppermute | solution.py:29
  216.6 13.8 %collective-permute-start = (f32[1,3,8,4096]{3,2,1,0:T(8,128)S(1)}, f32[1,3,8,4096]{3,2,1,0:T(8,128)S(1)}, u32[]{:S(2)}, u32[]{:S(2)}) collective-permute-start(f32[1,3,8,4096]{3,2,1,0:T(8,128)S(1)} %get-tuple-element.244), channel_id=1, source_target_pairs={{0,64},{64,128},{128,192},{192,256},{256,320},{320,384},{384,448},... | collective-permute-start | bytes 1179656 | tf_op jit(solution)/shard_map/while/body/eval_jaxpr/ppermute | solution.py:29
  230.4 11.4 %collective-permute-start = (f32[1,3,8,4096]{3,2,1,0:T(8,128)S(1)}, f32[1,3,8,4096]{3,2,1,0:T(8,128)S(1)}, u32[]{:S(2)}, u32[]{:S(2)}) collective-permute-start(f32[1,3,8,4096]{3,2,1,0:T(8,128)S(1)} %get-tuple-element.244), channel_id=1, source_target_pairs={{0,64},{64,128},{128,192},{192,256},{256,320},{320,384},{384,448},... | collective-permute-start | bytes 1179656 | tf_op jit(solution)/shard_map/while/body/eval_jaxpr/ppermute | solution.py:29
  241.9 11.3 %collective-permute-start = (f32[1,3,8,4096]{3,2,1,0:T(8,128)S(1)}, f32[1,3,8,4096]{3,2,1,0:T(8,128)S(1)}, u32[]{:S(2)}, u32[]{:S(2)}) collective-permute-start(f32[1,3,8,4096]{3,2,1,0:T(8,128)S(1)} %get-tuple-element.244), channel_id=1, source_target_pairs={{0,64},{64,128},{128,192},{192,256},{256,320},{320,384},{384,448},... | collective-permute-start | bytes 1179656 | tf_op jit(solution)/shard_map/while/body/eval_jaxpr/ppermute | solution.py:29
  253.3 11.6 %collective-permute-start = (f32[1,3,8,4096]{3,2,1,0:T(8,128)S(1)}, f32[1,3,8,4096]{3,2,1,0:T(8,128)S(1)}, u32[]{:S(2)}, u32[]{:S(2)}) collective-permute-start(f32[1,3,8,4096]{3,2,1,0:T(8,128)S(1)} %get-tuple-element.244), channel_id=1, source_target_pairs={{0,64},{64,128},{128,192},{192,256},{256,320},{320,384},{384,448},... | collective-permute-start | bytes 1179656 | tf_op jit(solution)/shard_map/while/body/eval_jaxpr/ppermute | solution.py:29
  265.0 14.3 %collective-permute-start = (f32[1,3,8,4096]{3,2,1,0:T(8,128)S(1)}, f32[1,3,8,4096]{3,2,1,0:T(8,128)S(1)}, u32[]{:S(2)}, u32[]{:S(2)}) collective-permute-start(f32[1,3,8,4096]{3,2,1,0:T(8,128)S(1)} %get-tuple-element.244), channel_id=1, source_target_pairs={{0,64},{64,128},{128,192},{192,256},{256,320},{320,384},{384,448},... | collective-permute-start | bytes 1179656 | tf_op jit(solution)/shard_map/while/body/eval_jaxpr/ppermute | solution.py:29
  279.3 13.0 %collective-permute-start.25 = (f32[1,3,8,4096]{3,2,1,0:T(8,128)S(1)}, f32[1,3,8,4096]{3,2,1,0:T(8,128)S(1)}, u32[]{:S(2)}, u32[]{:S(2)}) collective-permute-start(f32[1,3,8,4096]{3,2,1,0:T(8,128)S(1)} %get-tuple-element.55), channel_id=1, source_target_pairs={{0,64},{64,128},{128,192},{192,256},{256,320},{320,384},{384,448},... | collective-permute-start | bytes 1179656 | tf_op jit(solution)/shard_map/ppermute | solution.py:29
  (7 other events, 20.0 us)
where the time goes:
time: 294 us; the launch traced here: 293 us
  starting transfers between devices  133 us (45%)
  waiting for transfers between devices  116 us (39%)
  local copies, waits for them, and re-layouts  25.3 us (9%)
  matrix products  8.85 us (3%)
  other arithmetic  6.56 us (2%)
    ppermute x8, starting transfers between devices, passed_along(): lax.ppermute(shard, axis, [(i, (i + by) % size) for i in range(size)])  58.6 us
    ppermute x8, waiting for transfers between devices, passed_along(): lax.ppermute(shard, axis, [(i, (i + by) % size) for i in range(size)])  58.1 us
    ppermute x12, waiting for transfers between devices, padded(): lax.ppermute(lax.slice_in_dim(block, block.shape[dim] - width, None, axis...  57.9 us
    ppermute x12, starting transfers between devices, padded(): lax.ppermute(lax.slice_in_dim(block, block.shape[dim] - width, None, axis...  37.9 us
    ppermute x12, starting transfers between devices, padded(): lax.ppermute(lax.slice_in_dim(block, 0, width, axis=dim), axis, backward)  36.9 us
    dot_general x48, matrix products, take_edges(): jnp.dot(select, edges, precision=lax.Precision.HIGHEST, preferred_element...  8.85 us
    dynamic_slice x8, local copies, waits for them, and re-layouts, body(): depth = lax.map(depth_row, depth_level)  7.37 us
  transfers between devices with their start and end apart: 32, of which 20 were waited for; matrix products, arithmetic and copies ran while one was open for 3% of the time, Pallas kernels for 0%

commit v1 on v0

v1 whole, which is shorter than its diff:
```python
import functools
import math

import jax
import jax.numpy as jnp
import numpy as np
from jax import lax
from jax.experimental import pallas as pl
from jax.experimental.pallas import tpu as pltpu
from jax.sharding import PartitionSpec as P

BS = 64
STEPS = 6
SLICES = 8
NV = 32
CHUNK = 16
HALF = 48
PART = 12
MESH = pl.DeviceIdType.MESH


def lanes():
    return lax.broadcasted_iota(jnp.int32, (8, 128), 1)


def turn(x, by):
    return pltpu.roll(x, by % 128, axis=x.ndim - 1)


def permuted(x, index, valid):
    if x.ndim == 2:
        picked = jnp.take_along_axis(x, index, axis=0, mode="promise_in_bounds")
        return jnp.where(valid, picked, 0.0)
    return jnp.stack([permuted(x[i], index, valid) for i in range(x.shape[0])])


def kernel(
    n_space,
    start_hbm, gain_hbm, level_hbm, wet_hbm, cor_hbm, tide_hbm, table_ref, nb_ref, count_ref, trig_ref,
    out_ref,
    start, gain, lev, wet, cor, tide, table,
    depth_o, mask_o, t0_o, t1_o, c_o, eta_o, u_o, v_o, ry_o,
    depth_s, mask_s, t0_s, t1_s, c_s, eta_s, u_s, v_s, ry_s,
    pack_r, pack_l, got_r, got_l, nb_r, nb_l, nbgot_r, nbgot_l,
    eo, swap, cpart, cgot, xown, xgot, xsend, final,
    load_sem, hs_r, hr_r, hs_l, hr_l, nsem, chip_sem, cs, cr, xs, xr, fs, fr,
):
    m = lax.axis_index("tm")
    c = lax.axis_index("space")
    core = lax.rem(m, 2)
    chip = lax.div(m, 2)
    right = (m, lax.rem(c + 1, n_space))
    left = (m, lax.rem(c + n_space - 1, n_space))
    twin = (m + 1 - 2 * core, c)

    def chip_at(d):
        return (lax.rem(chip + d, 4) * 2 + core, c)

    barrier = pltpu.get_barrier_semaphore()
    peers = [right, left, twin, chip_at(1), chip_at(2), chip_at(3)]
    for peer in peers:
        pl.semaphore_signal(barrier, inc=1, device_id=peer, device_id_type=MESH)

    loads = []
    for j, (src, dst) in enumerate(
        [(wet_hbm, wet), (level_hbm, lev), (start_hbm, start), (cor_hbm, cor), (tide_hbm, tide), (gain_hbm, gain)]
    ):
        copy = pltpu.make_async_copy(src, dst, load_sem.at[j])
        copy.start()
        loads.append(copy)

    lane = lanes()
    low = lane < 64
    col = lane & 63
    group = (lane >> 4) & 3
    near = col < 32

    table[...] = jnp.zeros_like(table)
    table[:, 0:64] = jnp.broadcast_to(table_ref[...], (8, 64))
    nb = nb_ref[...]
    n_own, s_own, e_own, w_own = [jnp.broadcast_to(nb[:, j : j + 1], (8, 128)) for j in range(4)]
    for j, (to_right, to_left) in enumerate([(n_own, n_own), (s_own, s_own), (e_own, w_own)]):
        nb_r[j] = to_right
        nb_l[j] = to_left
    slot_live = lax.broadcasted_iota(jnp.int32, (8, 128), 0) < count_ref[0]

    def packed(value, into, k0):
        for q in range(value.shape[0] // 4):
            to_r = to_l = value[4 * q]
            for i in range(1, 4):
                turned = turn(value[4 * q + i], 16 * i)
                to_r = jnp.where(group == (i + 3) % 4, turned, to_r)
                to_l = jnp.where(group == i, turned, to_l)
            pack_r[into, k0 // 4 + q] = to_r
            pack_l[into, k0 // 4 + q] = to_l

    def halo(j):
        return (
            pltpu.make_async_remote_copy(
                pack_r.at[j], got_r.at[j], hs_r.at[j], hr_r.at[j], device_id=right, device_id_type=MESH
            ),
            pltpu.make_async_remote_copy(
                pack_l.at[j], got_l.at[j], hs_l.at[j], hr_l.at[j], device_id=left, device_id_type=MESH
            ),
        )

    n_copies = (
        pltpu.make_async_remote_copy(nb_r, nbgot_r, nsem.at[0], nsem.at[1], device_id=right, device_id_type=MESH),
        pltpu.make_async_remote_copy(nb_l, nbgot_l, nsem.at[2], nsem.at[3], device_id=left, device_id_type=MESH),
    )
    halos = [halo(j) for j in range(8)]
    chunks = range(0, NV, CHUNK)

    loads[0].wait()
    for k0 in chunks:
        ks = pl.ds(k0, CHUNK)
        live = jnp.where(jnp.logical_and(wet[ks] != 0, slot_live[None]), 0.15, 0.0)
        mask_o[ks] = live
        packed(live, 0, k0)
    loads[1].wait()
    entries = table[...]
    for k0 in chunks:
        ks = pl.ds(k0, CHUNK)
        index = lev[ks]
        depth = jnp.stack(
            [jnp.take_along_axis(entries, index[i], axis=1, mode="promise_in_bounds") for i in range(CHUNK)]
        )
        depth_o[ks] = depth
        packed(depth, 1, k0)
    pl.semaphore_wait(barrier, len(peers))
    for copy in n_copies:
        copy.start()
    for j in (0, 1):
        for copy in halos[j]:
            copy.start()
    loads[2].wait()
    for j, (field, state) in enumerate(((1, u_o), (2, v_o), (0, eta_o))):
        for k0 in chunks:
            ks = pl.ds(k0, CHUNK)
            value = jnp.where(mask_o[ks] > 0.0, start[field, ks], 0.0)
            start[field, ks] = value
            state[ks] = value
            packed(value, 2 + j, k0)
        for copy in halos[2 + j]:
            copy.start()
    loads[4].wait()
    for j, into in enumerate((t0_o, t1_o)):
        for k0 in chunks:
            ks = pl.ds(k0, CHUNK)
            value = (2.0 * mask_o[ks]) * tide[j, ks]
            into[ks] = value
            packed(value, 5 + j, k0)
        for copy in halos[5 + j]:
            copy.start()
    loads[3].wait()
    for k0 in chunks:
        ks = pl.ds(k0, CHUNK)
        value = 0.3 * cor[ks]
        c_o[ks] = value
        packed(value, 7, k0)
    for copy in halos[7]:
        copy.start()
    loads[5].wait()

    for copy in n_copies:
        copy.wait_recv()
    n_r, s_r, w_r = nbgot_l[0], nbgot_l[1], nbgot_l[2]
    n_l, s_l, e_l = nbgot_r[0], nbgot_r[1], nbgot_r[2]

    def lookup(index):
        return jnp.maximum(index, 0), index >= 0

    x_own = lookup(jnp.where(near, e_own, w_own))
    y_own = lookup(jnp.where(low, s_own, n_own))
    x_strip = lookup(jnp.where(near, e_l, w_r))
    y_strip = lookup(jnp.where(low, jnp.where(near, n_r, n_l), jnp.where(near, s_r, s_l)))

    for j, into in enumerate((mask_s, depth_s, u_s, v_s, eta_s, t0_s, t1_s, c_s)):
        for copy in halos[j]:
            copy.wait_recv()
        for q in range(NV // 4):
            from_l, from_r = got_r[j, q], got_l[j, q]
            for i in range(4):
                both = jnp.where(group == i, from_r, from_l)
                into[4 * q + i] = turn(both, 64 - 16 * i)

    first = col == 0
    last = col == 63

    def slope_x(own, strip):
        strip_at = permuted(strip, *x_own)
        own_at = permuted(own, *x_strip)
        d_own = turn(jnp.where(first, strip_at, own), -1) - turn(jnp.where(last, strip_at, own), 1)
        d_strip = turn(jnp.where(first, own_at, strip), -1) - turn(jnp.where(last, own_at, strip), 1)
        return d_own, d_strip

    def slope_y_own(k0):
        before, here, after = ry_o[pl.ds(k0, CHUNK)], ry_o[pl.ds(k0 + 1, CHUNK)], ry_o[pl.ds(k0 + 2, CHUNK)]
        return jnp.where(low, here, after) - jnp.where(low, before, here)

    def slope_y_strip(k0):
        before, here, after = ry_s[pl.ds(k0, CHUNK)], ry_s[pl.ds(k0 + 1, CHUNK)], ry_s[pl.ds(k0 + 2, CHUNK)]
        return jnp.where(low, after, here) - jnp.where(low, here, before)

    def ends(strip):
        ends_own = permuted(jnp.where(low, ry_o[NV], ry_o[1]), *y_own)
        ry_o[0] = ends_own
        ry_o[NV + 1] = ends_own
        if strip:
            ends_strip = permuted(jnp.where(low, ry_s[1], ry_s[NV]), *y_strip)
            ry_s[0] = ends_strip
            ry_s[NV + 1] = ends_strip

    for k0 in chunks:
        ks, up = pl.ds(k0, CHUNK), pl.ds(k0 + 1, CHUNK)
        ry_o[up] = turn(depth_o[ks] * v_o[ks], 64)
        ry_s[up] = turn(depth_s[ks] * v_s[ks], 64)
    ends(True)

    def surface(step):
        cosine = trig_ref[m * STEPS + step]
        sine = trig_ref[SLICES * STEPS + m * STEPS + step]
        keep = []
        for k0 in chunks:
            ks = pl.ds(k0, CHUNK)
            dx_o, dx_s = slope_x(depth_o[ks] * u_o[ks], depth_s[ks] * u_s[ks])
            for eta, mask, t0, t1, dx, dy in (
                (eta_o, mask_o, t0_o, t1_o, dx_o, slope_y_own(k0)),
                (eta_s, mask_s, t0_s, t1_s, dx_s, slope_y_strip(k0)),
            ):
                eta[ks] = eta[ks] + (t0[ks] * cosine + t1[ks] * sine) - mask[ks] * (dx + dy)
        for k0 in chunks:
            ks, up = pl.ds(k0, CHUNK), pl.ds(k0 + 1, CHUNK)
            ry_o[up] = turn(eta_o[ks], 64)
            ry_s[up] = turn(eta_s[ks], 64)
        ends(True)

    def one_step(step, carry):
        surface(step)
        for k0 in chunks:
            ks = pl.ds(k0, CHUNK)
            dx_o, dx_s = slope_x(eta_o[ks], eta_s[ks])
            for u_ref, v_ref, mask, cc, dx, dy in (
                (u_o, v_o, mask_o, c_o, dx_o, slope_y_own(k0)),
                (u_s, v_s, mask_s, c_s, dx_s, slope_y_strip(k0)),
            ):
                u, v = u_ref[ks], v_ref[ks]
                u_ref[ks] = 0.985 * u + cc[ks] * jnp.where(mask[ks] > 0.0, v, 0.0) - mask[ks] * dx
                v_ref[ks] = 0.985 * v - cc[ks] * jnp.where(mask[ks] > 0.0, u, 0.0) - mask[ks] * dy
        for k0 in chunks:
            ks, up = pl.ds(k0, CHUNK), pl.ds(k0 + 1, CHUNK)
            ry_o[up] = turn(depth_o[ks] * v_o[ks], 64)
            ry_s[up] = turn(depth_s[ks] * v_s[ks], 64)
        ends(True)
        return carry

    lax.fori_loop(0, STEPS - 1, one_step, 0)
    surface(STEPS - 1)

    def defect(field, ks, fine):
        return fine - gain[field, ks] * start[field, ks]

    for k0 in chunks:
        ks = pl.ds(k0, CHUNK)
        final[0, pl.ds(k0, CHUNK)] = defect(0, ks, eta_o[ks])
        dx, _ = slope_x(eta_o[ks], eta_s[ks])
        dy = slope_y_own(k0)
        u, v = u_o[ks], v_o[ks]
        new_u = 0.985 * u + c_o[ks] * v - mask_o[ks] * dx
        new_v = 0.985 * v - c_o[ks] * u - mask_o[ks] * dy
        half, at = divmod(NV + k0, HALF)
        final[half, pl.ds(at, CHUNK)] = defect(1, ks, new_u)
        final[1, pl.ds(16 + k0, CHUNK)] = defect(2, ks, new_v)

    swap_copy = pltpu.make_async_remote_copy(
        final.at[1 - core], eo.at[core], chip_sem.at[0], chip_sem.at[1], device_id=twin, device_id_type=MESH
    )
    swap_copy.start()
    eo[core] = final[core]
    swap_copy.wait_recv()

    def gain_of(p):
        return swap[pl.ds(p * PART, PART)]

    @pl.when(core == 0)
    def _():
        swap[pl.ds(0, NV)] = gain[0]
        swap[pl.ds(NV, 16)] = gain[1, 0:16]

    @pl.when(core == 1)
    def _():
        swap[pl.ds(0, 16)] = gain[1, 16:32]
        swap[pl.ds(16, NV)] = gain[2]

    c_copies = {}
    for d in (2, 1, 3, 0):
        p = lax.rem(chip + d, 4)
        ps = pl.ds(p * PART, PART)
        cpart[d] = eo[1, ps] + gain_of(p) * eo[0, ps]
        if d:
            c_copies[d] = pltpu.make_async_remote_copy(
                cpart.at[d], cgot.at[d], cs.at[d], cr.at[d], device_id=chip_at(d), device_id_type=MESH
            )
            c_copies[d].start()

    g = gain_of(chip)
    g2 = g * g
    g4 = g2 * g2
    inverse = 1.0 / (1.0 - g4 * g4)
    for d in (1, 3, 2):
        c_copies[d].wait_recv()
    own = cpart[0]
    x = (cgot[1] + g2 * (cgot[2] + g2 * (cgot[3] + g2 * own))) * inverse
    xown[...] = x
    x1 = own + g2 * x
    x2 = cgot[3] + g2 * x1
    x3 = cgot[2] + g2 * x2
    x_copies = {}
    for d, value in ((2, x2), (1, x1), (3, x3)):
        xsend[d] = value
        x_copies[d] = pltpu.make_async_remote_copy(
            xsend.at[d], xgot.at[d], xs.at[d], xr.at[d], device_id=chip_at(d), device_id_type=MESH
        )
        x_copies[d].start()

    f_copies = []
    for d in (0, 1, 3, 2):
        if d:
            x_copies[d].wait_recv()
        p = lax.rem(chip + 4 - d, 4)
        ps = pl.ds(p * PART, PART)
        even = xgot[d] if d else xown[...]
        odd = gain_of(p) * even + eo[0, ps]
        mine = jnp.where(core == 0, even, odd)
        other = jnp.where(core == 0, odd, even)
        cpart[4 + d] = other
        at = pl.ds(core * HALF + p * PART, PART)
        copy = pltpu.make_async_remote_copy(
            cpart.at[4 + d], out_ref.at[at], fs.at[d], fr.at[d], device_id=twin, device_id_type=MESH
        )
        copy.start()
        f_copies.append(copy)
        out_ref[at] = mine
    for copy in f_copies:
        copy.wait()

    for pair in halos:
        for copy in pair:
            copy.wait_send()
    for copy in n_copies:
        copy.wait_send()
    swap_copy.wait_send()
    for d in (1, 2, 3):
        c_copies[d].wait_send()
        x_copies[d].wait_send()


def by_vreg(x):
    split = x.reshape(x.shape[:-1] + (NV, 128))
    return jnp.swapaxes(split, -3, -2)


def body(n_space, start_states, coarse_gain, depth_level, depth_table, wet, block_count, neighbour, coriolis, tide):
    angles = np.arange(SLICES * STEPS) * (2.0 * math.pi / (SLICES * STEPS))
    trig = jnp.asarray(np.concatenate([np.cos(angles), np.sin(angles)]).astype(np.float32))
    f32, i32 = jnp.float32, jnp.int32
    field = pltpu.VMEM((NV, 8, 128), f32)
    field_i = pltpu.VMEM((NV, 8, 128), i32)
    state = pltpu.VMEM((3, NV, 8, 128), f32)
    edge = pltpu.VMEM((8, NV // 4, 8, 128), f32)
    rows = pltpu.VMEM((NV + 2, 8, 128), f32)
    vmem, anywhere, smem = (
        pl.BlockSpec(memory_space=pltpu.VMEM),
        pl.BlockSpec(memory_space=pl.ANY),
        pl.BlockSpec(memory_space=pltpu.SMEM),
    )
    dma = pltpu.SemaphoreType.DMA
    fields = [field] * 8 + [rows]
    out = pl.pallas_call(
        functools.partial(kernel, n_space),
        out_shape=jax.ShapeDtypeStruct((3 * NV, 8, 128), f32),
        in_specs=[anywhere] * 6 + [vmem, vmem, smem, smem],
        out_specs=vmem,
        scratch_shapes=[state, state, field_i, field_i, field, pltpu.VMEM((2, NV, 8, 128), f32), pltpu.VMEM((8, 128), f32)]
        + fields
        + fields
        + [edge] * 4
        + [pltpu.VMEM((3, 8, 128), i32)] * 4
        + [
            pltpu.VMEM((2, HALF, 8, 128), f32),
            pltpu.VMEM((HALF, 8, 128), f32),
            pltpu.VMEM((8, PART, 8, 128), f32),
            pltpu.VMEM((4, PART, 8, 128), f32),
            pltpu.VMEM((PART, 8, 128), f32),
            pltpu.VMEM((4, PART, 8, 128), f32),
            pltpu.VMEM((4, PART, 8, 128), f32),
            pltpu.VMEM((2, HALF, 8, 128), f32),
        ]
        + [dma((6,)), dma((8,)), dma((8,)), dma((8,)), dma((8,)), dma((4,)), dma((2,))]
        + [dma((4,))] * 6,
        compiler_params=pltpu.CompilerParams(
            collective_id=0, has_side_effects=True, vmem_limit_bytes=32 * 1024 * 1024
        ),
    )(
        by_vreg(start_states)[0],
        by_vreg(coarse_gain),
        by_vreg(depth_level),
        by_vreg(wet),
        by_vreg(coriolis),
        by_vreg(tide),
        depth_table.reshape(1, 64),
        neighbour,
        block_count,
        trig,
    )
    out = out.reshape(3, NV, 8, 128)
    return jnp.swapaxes(out, 1, 2).reshape(1, 3, 8, NV * 128)


def solution(mesh):
    return jax.shard_map(
        functools.partial(body, mesh.shape["space"]),
        mesh=mesh,
        in_specs=(
            P("tm", None, "space", None),
            P(None, "space", None),
            P("space", None),
            P(),
            P("space", None),
            P("space"),
            P("space", None),
            P("space", None),
            P(None, "space", None),
        ),
        out_specs=P("tm", None, "space", None),
        check_vma=False,
    )
```

time: 294 us -> 51.8 us (0.18)
  starting transfers between devices: 133 us -> 0 us
  waiting for transfers between devices: 116 us -> 0 us
  Pallas kernels: 0 us -> 43.1 us
  local copies, waits for them, and re-layouts: 25.3 us -> 7.74 us
  matrix products: 8.85 us -> 0 us
  other arithmetic: 6.56 us -> 0 us
    ppermute x32 -> x0, starting transfers between devices: 133 us -> none  [the longest x8 58.6 us: passed_along(): lax.ppermute(shard, axis, [(i, (i + by) % size) for i in range(size)])]
    ppermute x32 -> x0, waiting for transfers between devices: 116 us -> none  [the longest x8 58.1 us: passed_along(): lax.ppermute(shard, axis, [(i, (i + by) % size) for i in range(size)])]
    pallas_call x0 -> x1, Pallas kernels: none -> 43.1 us  [body(): pl.pallas_call(functools.partial(kernel, n_space), out_shape=jax.ShapeDty...]
    dot_general x48 -> x0, matrix products: 8.85 us -> none  [take_edges(): jnp.dot(select, edges, precision=lax.Precision.HIGHEST, preferred_element...]
    dynamic_slice x8 -> x0, local copies, waits for them, and re-layouts: 7.37 us -> none  [body(): depth = lax.map(depth_row, depth_level)]
    slice x48 -> x0, local copies, waits for them, and re-layouts: 5.61 us -> none  [the longest x24 3.33 us: edge_pair(): return jnp.stack([field[:, 0::BS], field[:, BS - 1::BS]])]
    unnamed x15 -> x20, local copies, waits for them, and re-layouts: 3.19 us -> 7.74 us
    broadcast_in_dim x24 -> x0, local copies, waits for them, and re-layouts: 3.2 us -> none  [the longest x12 1.6 us: across(): jnp.repeat(west_ghost, BS, axis=-1)]
  transfers between devices with their start and end apart: 32 -> 0, of which waited for: 20 -> 0; matrix products, arithmetic and copies ran while one was open for 3% -> 0% of each run, Pallas kernels for 0% -> 0%
where the time goes in v1:
time: 51.8 us; the launch traced here: 51.5 us
  Pallas kernels  43.1 us (83%)
  local copies, waits for them, and re-layouts  7.74 us (15%)
  between operations  0.68 us (1%)
    pallas_call x1, Pallas kernels, body(): pl.pallas_call(functools.partial(kernel, n_space), out_shape=jax.ShapeDty...  43.1 us
    unnamed x20, local copies, waits for them, and re-layouts  7.74 us

profile of v1, /device:TPU:1, one launch (start us, length us, event | category | flops | bytes accessed | tf_op | source)
XLA Modules:
  0.0 51.5 jit_solution(1437302359475431742)
XLA Ops:
  0.7 0.0 copy-start.8
  0.7 0.7 %copy-done.8 = s32[8,4]{0,1:T(4,128)S(1)} copy-done((s32[8,4]{0,1:T(4,128)S(1)}, s32[8,4]{0,1:T(4,128)}, u32[]{:S(2)}) %copy-start.8) | copy-done | bytes 152
  1.3 0.0 copy-start.6
  1.3 0.0 copy-start.7
  1.3 0.1 copy.11.nb_ref
  1.4 0.6 %copy-done.6 = f32[64]{0:T(128)S(1)} copy-done((f32[64]{0:T(128)S(1)}, f32[64]{0:T(128)}, u32[]{:S(2)}) %copy-start.6) | copy-done | bytes 280
  2.0 0.0 copy-done.7
  2.0 0.0 copy-start
  2.0 1.0 %copy-done = f32[1,3,8,4096]{3,2,1,0:T(8,128)S(1)} copy-done((f32[1,3,8,4096]{3,2,1,0:T(8,128)S(1)}, f32[1,3,8,4096]{3,2,1,0:T(8,128)}, u32[]{:S(2)}) %copy-start) | copy-done | bytes 393240
  3.0 0.0 copy-start.1
  3.0 1.0 %copy-done.1 = f32[3,8,4096]{2,1,0:T(8,128)S(1)} copy-done((f32[3,8,4096]{2,1,0:T(8,128)S(1)}, f32[3,8,4096]{2,1,0:T(8,128)}, u32[]{:S(2)}) %copy-start.1) | copy-done | bytes 393240
  4.0 0.0 copy-start.2
  4.0 0.9 %copy-done.2 = f32[2,8,4096]{2,1,0:T(8,128)S(1)} copy-done((f32[2,8,4096]{2,1,0:T(8,128)S(1)}, f32[2,8,4096]{2,1,0:T(8,128)}, u32[]{:S(2)}) %copy-start.2) | copy-done | bytes 262168
  5.0 0.0 copy-start.3
  5.0 0.9 %copy-done.3 = s32[8,4096]{1,0:T(8,128)S(1)} copy-done((s32[8,4096]{1,0:T(8,128)S(1)}, s32[8,4096]{1,0:T(8,128)}, u32[]{:S(2)}) %copy-start.3) | copy-done | bytes 131096
  5.9 0.0 copy-start.4
  5.9 0.9 %copy-done.4 = s32[8,4096]{1,0:T(8,128)S(1)} copy-done((s32[8,4096]{1,0:T(8,128)S(1)}, s32[8,4096]{1,0:T(8,128)}, u32[]{:S(2)}) %copy-start.4) | copy-done | bytes 131096
  6.8 0.0 copy-start.5
  6.8 0.9 %copy-done.5 = f32[8,4096]{1,0:T(8,128)S(1)} copy-done((f32[8,4096]{1,0:T(8,128)S(1)}, f32[8,4096]{1,0:T(8,128)}, u32[]{:S(2)}) %copy-start.5) | copy-done | bytes 131096
  7.7 43.1 %shard_map.100 = f32[96,8,128]{2,1,0:T(8,128)S(1)} custom-call(f32[3,32,8,128]{3,2,1,0:T(8,128)S(1)} %bitcast.27, f32[3,32,8,128]{3,2,1,0:T(8,128)S(1)} %bitcast.28, s32[32,8,128]{2,1,0:T(8,128)S(1)} %bitcast.30, s32[32,8,128]{2,1,0:T(8,128)S(1)} %bitcast.31, f32[32,8,128]{2,1,0:T(8,128)S(1)} %bitcast.32, f32[2,32,8,128]{3,2,1,0:T(8,128)S(1)} %bitcast.29, ...), custom_call_target="tpu_custom_call" | custom-call | tf_op jit(solution)/shard_map/pallas_call | solution.py:379
  50.8 0.7 %copy.14 = f32[1,3,8,4096]{3,2,1,0:T(8,128)} copy(f32[1,3,8,4096]{3,2,1,0:T(8,128)S(1)} %bitcast.26) | data formatting | bytes 786432
Async XLA Ops:
  0.7 0.7 %copy-start.8 = (s32[8,4]{0,1:T(4,128)S(1)}, s32[8,4]{0,1:T(4,128)}, u32[]{:S(2)}) copy-start(s32[8,4]{0,1:T(4,128)} %param.16) | copy-start | bytes 388
  1.3 0.7 %copy-start.6 = (f32[64]{0:T(128)S(1)}, f32[64]{0:T(128)}, u32[]{:S(2)}) copy-start(f32[64]{0:T(128)} %param.13) | copy-start | bytes 772
  1.3 0.7 %copy-start.7 = (f32[96]{0:T(128)S(1)}, f32[96]{0:T(128)}, u32[]{:S(2)}) copy-start(f32[96]{0:T(128)} %constant.2.clone.trig_ref) | copy-start | bytes 1156
  2.0 1.0 %copy-start = (f32[1,3,8,4096]{3,2,1,0:T(8,128)S(1)}, f32[1,3,8,4096]{3,2,1,0:T(8,128)}, u32[]{:S(2)}) copy-start(f32[1,3,8,4096]{3,2,1,0:T(8,128)} %param.10) | copy-start | bytes 1179652
  3.0 1.0 %copy-start.1 = (f32[3,8,4096]{2,1,0:T(8,128)S(1)}, f32[3,8,4096]{2,1,0:T(8,128)}, u32[]{:S(2)}) copy-start(f32[3,8,4096]{2,1,0:T(8,128)} %param.11) | copy-start | bytes 1179652
  4.0 0.9 %copy-start.2 = (f32[2,8,4096]{2,1,0:T(8,128)S(1)}, f32[2,8,4096]{2,1,0:T(8,128)}, u32[]{:S(2)}) copy-start(f32[2,8,4096]{2,1,0:T(8,128)} %param.18) | copy-start | bytes 786436
  5.0 0.9 %copy-start.3 = (s32[8,4096]{1,0:T(8,128)S(1)}, s32[8,4096]{1,0:T(8,128)}, u32[]{:S(2)}) copy-start(s32[8,4096]{1,0:T(8,128)} %param.12) | copy-start | bytes 393220
  5.9 0.9 %copy-start.4 = (s32[8,4096]{1,0:T(8,128)S(1)}, s32[8,4096]{1,0:T(8,128)}, u32[]{:S(2)}) copy-start(s32[8,4096]{1,0:T(8,128)} %param.14) | copy-start | bytes 393220
  6.8 0.9 %copy-start.5 = (f32[8,4096]{1,0:T(8,128)S(1)}, f32[8,4096]{1,0:T(8,128)}, u32[]{:S(2)}) copy-start(f32[8,4096]{1,0:T(8,128)} %param.17) | copy-start | bytes 393220

commit v2 on v1

v2 whole, which is shorter than its diff:
```python
import functools
import math

import jax
import jax.numpy as jnp
from jax import lax
from jax.experimental import pallas as pl
from jax.experimental.pallas import tpu as pltpu
from jax.sharding import PartitionSpec as P

STEPS = 6
SLICES = 8
LEVELS = 64
NV = 32
FIXED = 5
CHUNK = 16
MESH = pl.DeviceIdType.MESH


def lanes():
    return lax.broadcasted_iota(jnp.int32, (8, 128), 1)


def turn(x, by):
    return pltpu.roll(x, by % 128, axis=x.ndim - 1)


def permuted(x, index, valid):
    if x.ndim == 2:
        picked = jnp.take_along_axis(x, index, axis=0, mode="promise_in_bounds")
        return jnp.where(valid, picked, 0.0)
    return jnp.stack([permuted(x[i], index, valid) for i in range(x.shape[0])])


def kernel(
    n_space,
    start_hbm, gain_hbm, level_hbm, wet_hbm, cor_hbm, tide_hbm, table_hbm, nb_hbm, count_hbm,
    out_ref,
    start, gain, lev, wet, cor, tide, table, nb, count, trig,
    depth_o, mask_o, t0_o, t1_o, c_o, eta_o, u_o, v_o, rf_o, re_o,
    depth_s, mask_s, t0_s, t1_s, c_s, eta_s, u_s, v_s, rf_s, re_s,
    pack_r, pack_l, got_r, got_l, nb_r, nb_l, nbgot_r, nbgot_l,
    eo, swap, cpart, cgot, xpart, xgot, final,
    load_sem, hs_r, hr_r, hs_l, hr_l, nsem, os, orr, ss, sr, cs, cr, xs, xr, fs, fr,
):
    m = lax.axis_index("tm")
    c = lax.axis_index("space")
    core = lax.rem(m, 2)
    chip = lax.div(m, 2)
    right = (m, lax.rem(c + 1, n_space))
    left = (m, lax.rem(c + n_space - 1, n_space))
    twin = (m + 1 - 2 * core, c)

    def chip_at(d):
        return (lax.rem(chip + d, 4) * 2 + core, c)

    barrier = pltpu.get_barrier_semaphore()
    peers = [right, left, twin, chip_at(1), chip_at(2), chip_at(3)]
    for peer in peers:
        pl.semaphore_signal(barrier, inc=1, device_id=peer, device_id_type=MESH)

    loads = []
    for j, (src, dst) in enumerate(
        [
            (wet_hbm, wet),
            (level_hbm, lev),
            (start_hbm, start),
            (cor_hbm, cor),
            (tide_hbm, tide),
            (gain_hbm, gain),
            (count_hbm, count),
            (nb_hbm, nb),
            (table_hbm, table),
        ]
    ):
        loads.append(pltpu.make_async_copy(src, dst, load_sem.at[j]))
    for j in (3, 6, 0, 4, 8, 1, 2, 7, 5):
        loads[j].start()

    lane = lanes()
    low = lane < 64
    col = lane & 63
    group = (lane >> 4) & 3
    near = col < 32

    slot = lax.broadcasted_iota(jnp.int32, (8, 128), 0)

    def packed(value, into, q0):
        for q in range(value.shape[0] // 4):
            to_r = to_l = value[4 * q]
            for i in range(1, 4):
                turned = turn(value[4 * q + i], 16 * i)
                to_r = jnp.where(group == (i + 3) % 4, turned, to_r)
                to_l = jnp.where(group == i, turned, to_l)
            pack_r[into, q0 + q] = to_r
            pack_l[into, q0 + q] = to_l

    def halo(j):
        at = pl.ds(4 * core, 4) if j < FIXED else pl.ds(0, 8)
        return (
            pltpu.make_async_remote_copy(
                pack_r.at[j, at], got_r.at[j, at], hs_r.at[j], hr_r.at[j], device_id=right, device_id_type=MESH
            ),
            pltpu.make_async_remote_copy(
                pack_l.at[j, at], got_l.at[j, at], hs_l.at[j], hr_l.at[j], device_id=left, device_id_type=MESH
            ),
        )

    def onward(j):
        at = pl.ds(4 * core, 4)
        return [
            pltpu.make_async_remote_copy(
                got.at[j, at], got.at[j, at], os.at[i, j], orr.at[i, j], device_id=twin, device_id_type=MESH
            )
            for i, got in enumerate((got_r, got_l))
        ]

    n_copies = (
        pltpu.make_async_remote_copy(nb_r, nbgot_r, nsem.at[0], nsem.at[1], device_id=right, device_id_type=MESH),
        pltpu.make_async_remote_copy(nb_l, nbgot_l, nsem.at[2], nsem.at[3], device_id=left, device_id_type=MESH),
    )
    halos = [halo(j) for j in range(8)]
    chunks = range(0, NV, CHUNK)

    def send(j):
        for copy in halos[j]:
            copy.start()

    def fixed(j, into, value_of):
        for half in (core, 1 - core):
            ks = pl.ds(half * CHUNK, CHUNK)
            value = value_of(ks)
            into[ks] = value
            if half is core:
                packed(value, j, 4 * core)
                if j == 0:
                    pl.semaphore_wait(barrier, len(peers))
                for copy in halos[j]:
                    copy.start()

    def depth_of(ks):
        index = lev[ks]
        return jnp.stack(
            [jnp.take_along_axis(entries, index[i], axis=1, mode="promise_in_bounds") for i in range(CHUNK)]
        )

    loads[3].wait()
    fixed(0, c_o, lambda ks: 0.3 * cor[ks])
    loads[6].wait()
    slot_live = slot < count[0]
    loads[0].wait()
    fixed(1, mask_o, lambda ks: jnp.where(jnp.logical_and(wet[ks] != 0, slot_live[None]), 0.15, 0.0))
    loads[4].wait()
    fixed(2, t0_o, lambda ks: (2.0 * mask_o[ks]) * tide[0, ks])
    fixed(3, t1_o, lambda ks: (2.0 * mask_o[ks]) * tide[1, ks])
    loads[1].wait()
    loads[8].wait()
    entries = jnp.full((8, 128), table[0])
    for n in range(1, LEVELS):
        entries = jnp.where(lane == n, table[n], entries)
    fixed(4, depth_o, depth_of)
    loads[2].wait()
    for j, (field, state) in enumerate(((1, u_o), (2, v_o), (0, eta_o))):
        for k0 in chunks:
            ks = pl.ds(k0, CHUNK)
            value = jnp.where(mask_o[ks] > 0.0, start[field, ks], 0.0)
            start[field, ks] = value
            state[ks] = value
            packed(value, FIXED + j, k0 // 4)
        for copy in halos[FIXED + j]:
            copy.start()
    loads[7].wait()
    def by_slot(side):
        entry = jnp.full((8, 128), nb[side, 0])
        for s in range(1, 8):
            entry = jnp.where(slot == s, nb[side, s], entry)
        return entry

    n_own, s_own, e_own, w_own = [by_slot(j) for j in range(4)]
    for j, (to_right, to_left) in enumerate([(n_own, n_own), (s_own, s_own), (e_own, w_own)]):
        nb_r[j] = to_right
        nb_l[j] = to_left
    for copy in n_copies:
        copy.start()
    for j in range(STEPS):
        for at, wave in ((0, math.cos), (STEPS, math.sin)):
            value = jnp.float32(0.0)
            for n in range(SLICES):
                value = jnp.where(m == n, jnp.float32(wave((n * STEPS + j) * (2.0 * math.pi / (SLICES * STEPS)))), value)
            trig[at + j] = value
    loads[5].wait()

    onwards = [onward(j) for j in range(FIXED)]
    for j in range(FIXED):
        for copy, further in zip(halos[j], onwards[j]):
            copy.wait_recv()
            further.start()
    for j, into in enumerate((c_s, mask_s, t0_s, t1_s, depth_s, u_s, v_s, eta_s)):
        for copy in onwards[j] if j < FIXED else halos[j]:
            copy.wait_recv()
        for q in range(NV // 4):
            from_l, from_r = got_r[j, q], got_l[j, q]
            for i in range(4):
                both = jnp.where(group == i, from_r, from_l)
                into[4 * q + i] = turn(both, 64 - 16 * i)

    for copy in n_copies:
        copy.wait_recv()
    n_r, s_r, w_r = nbgot_l[0], nbgot_l[1], nbgot_l[2]
    n_l, s_l, e_l = nbgot_r[0], nbgot_r[1], nbgot_r[2]

    def lookup(index):
        return jnp.maximum(index, 0), index >= 0

    x_own = lookup(jnp.where(near, e_own, w_own))
    y_own = lookup(jnp.where(low, s_own, n_own))
    x_strip = lookup(jnp.where(near, e_l, w_r))
    y_strip = lookup(jnp.where(low, jnp.where(near, n_r, n_l), jnp.where(near, s_r, s_l)))

    first = col == 0
    last = col == 63

    def slope_x(own, strip, both=True):
        strip_at = permuted(strip, *x_own)
        d_own = turn(jnp.where(first, strip_at, own), -1) - turn(jnp.where(last, strip_at, own), 1)
        if not both:
            return d_own, None
        own_at = permuted(own, *x_strip)
        d_strip = turn(jnp.where(first, own_at, strip), -1) - turn(jnp.where(last, own_at, strip), 1)
        return d_own, d_strip

    def slope_y(rows, k0, size, swapped):
        step = rows[pl.ds(k0 + 1, size + 1)] - rows[pl.ds(k0, size + 1)]
        here, after = step[:size], step[1:]
        return jnp.where(low, after, here) if swapped else jnp.where(low, here, after)

    def ends(rows, swapped):
        if swapped:
            edge = permuted(jnp.where(low, rows[1], rows[NV]), *y_strip)
        else:
            edge = permuted(jnp.where(low, rows[NV], rows[1]), *y_own)
        rows[0] = edge
        rows[NV + 1] = edge

    for k0 in chunks:
        ks, up = pl.ds(k0, CHUNK), pl.ds(k0 + 1, CHUNK)
        rf_o[up] = turn(depth_o[ks] * v_o[ks], 64)
        rf_s[up] = turn(depth_s[ks] * v_s[ks], 64)
    ends(rf_o, False)
    ends(rf_s, True)

    def surface(step, more):
        cosine, sine = trig[step], trig[STEPS + step]
        for k0 in chunks:
            ks, up = pl.ds(k0, CHUNK), pl.ds(k0 + 1, CHUNK)
            dx_o, dx_s = slope_x(depth_o[ks] * u_o[ks], depth_s[ks] * u_s[ks])
            for eta, mask, t0, t1, dx, dy, rows, turned in (
                (eta_o, mask_o, t0_o, t1_o, dx_o, slope_y(rf_o, k0, CHUNK, False), re_o, True),
                (eta_s, mask_s, t0_s, t1_s, dx_s, slope_y(rf_s, k0, CHUNK, True), re_s, more),
            ):
                value = eta[ks] + (t0[ks] * cosine + t1[ks] * sine) - mask[ks] * (dx + dy)
                eta[ks] = value
                if turned:
                    rows[up] = turn(value, 64)
        ends(re_o, False)
        if more:
            ends(re_s, True)

    def one_step(step, carry):
        surface(step, True)
        for k0 in chunks:
            ks, up = pl.ds(k0, CHUNK), pl.ds(k0 + 1, CHUNK)
            dx_o, dx_s = slope_x(eta_o[ks], eta_s[ks])
            for u_ref, v_ref, mask, cc, depth, dx, dy, rows in (
                (u_o, v_o, mask_o, c_o, depth_o, dx_o, slope_y(re_o, k0, CHUNK, False), rf_o),
                (u_s, v_s, mask_s, c_s, depth_s, dx_s, slope_y(re_s, k0, CHUNK, True), rf_s),
            ):
                u, v = u_ref[ks], v_ref[ks]
                u_ref[ks] = 0.985 * u + cc[ks] * v - mask[ks] * dx
                new_v = 0.985 * v - cc[ks] * u - mask[ks] * dy
                v_ref[ks] = new_v
                rows[up] = turn(depth[ks] * new_v, 64)
        ends(rf_o, False)
        ends(rf_s, True)
        return carry

    lax.fori_loop(0, STEPS - 1, one_step, 0)
    surface(STEPS - 1, False)

    def rows_of(half, s):
        return pl.ds(half * 16 + 8 * s, 8)

    def defect(half, s):
        k0 = half * 16 + 8 * s
        ks = pl.ds(k0, 8)
        dx, _ = slope_x(eta_o[ks], eta_s[ks], False)
        dy = slope_y(re_o, k0, 8, False)
        u, v = u_o[ks], v_o[ks]
        fine = (
            eta_o[ks],
            0.985 * u + c_o[ks] * v - mask_o[ks] * dx,
            0.985 * v - c_o[ks] * u - mask_o[ks] * dy,
        )
        return [fine[f] - gain[f, ks] * start[f, ks] for f in range(3)]

    swaps, c_copies, x_copies, f_copies = {}, {}, {}, []
    for s in range(2):
        for f, value in enumerate(defect(1 - core, s)):
            swap[s, f] = value
        swaps[s] = pltpu.make_async_remote_copy(
            swap.at[s], eo.at[core, s], ss.at[s], sr.at[s], device_id=twin, device_id_type=MESH
        )
        swaps[s].start()
    for s in range(2):
        for f, value in enumerate(defect(core, s)):
            eo[core, s, f] = value

    def quarter(d):
        return pl.ds(2 * lax.rem(chip + d, 4), 2)

    for s in range(2):
        swaps[s].wait_recv()
        cpart[s] = eo[1, s] + gain[:, rows_of(core, s)] * eo[0, s]
        for d in (2, 1, 3):
            c_copies[d, s] = pltpu.make_async_remote_copy(
                cpart.at[s, :, quarter(d)], cgot.at[d, s], cs.at[d, s], cr.at[d, s],
                device_id=chip_at(d), device_id_type=MESH,
            )
            c_copies[d, s].start()

    for s in range(2):
        g = gain[:, pl.ds(core * 16 + 8 * s + 2 * chip, 2)]
        g2 = g * g
        g4 = g2 * g2
        inverse = 1.0 / (1.0 - g4 * g4)
        for d in (1, 3, 2):
            c_copies[d, s].wait_recv()
        own = cpart[s, :, quarter(0)]
        x = (cgot[1, s] + g2 * (cgot[2, s] + g2 * (cgot[3, s] + g2 * own))) * inverse
        x1 = own + g2 * x
        x2 = cgot[3, s] + g2 * x1
        x3 = cgot[2, s] + g2 * x2
        for d, value in ((2, x2), (1, x1), (3, x3)):
            xpart[d, s] = value
            x_copies[d, s] = pltpu.make_async_remote_copy(
                xpart.at[d, s], xgot.at[s, :, quarter(0)], xs.at[d, s], xr.at[d, s],
                device_id=chip_at(d), device_id_type=MESH,
            )
            x_copies[d, s].start()
        xgot[s, :, quarter(0)] = x

    for s in range(2):
        for d in (1, 3, 2):
            x_copies[d, s].wait_recv()
        even = xgot[s]
        odd = gain[:, rows_of(core, s)] * even + eo[0, s]
        final[s] = jnp.where(core == 0, odd, even)
        at = rows_of(core, s)
        copy = pltpu.make_async_remote_copy(
            final.at[s], out_ref.at[:, at], fs.at[s], fr.at[s], device_id=twin, device_id_type=MESH
        )
        copy.start()
        f_copies.append(copy)
        out_ref[:, at] = jnp.where(core == 0, even, odd)
    for copy in f_copies:
        copy.wait()

    for pair in onwards:
        for copy in pair:
            copy.wait_send()
    for copies in (swaps, c_copies, x_copies):
        for copy in copies.values():
            copy.wait_send()
    for pair in halos:
        for copy in pair:
            copy.wait_send()
    for copy in n_copies:
        copy.wait_send()


def by_vreg(x):
    split = x.reshape(x.shape[:-1] + (NV, 128))
    return jnp.swapaxes(split, -3, -2)


def body(n_space, start_states, coarse_gain, depth_level, depth_table, wet, block_count, neighbour, coriolis, tide):
    f32, i32 = jnp.float32, jnp.int32
    field = pltpu.VMEM((NV, 8, 128), f32)
    field_i = pltpu.VMEM((NV, 8, 128), i32)
    state = pltpu.VMEM((3, NV, 8, 128), f32)
    edge = pltpu.VMEM((8, NV // 4, 8, 128), f32)
    rows = pltpu.VMEM((NV + 2, 8, 128), f32)
    vmem, hbm = (
        pl.BlockSpec(memory_space=pltpu.VMEM),
        pl.BlockSpec(memory_space=pltpu.HBM),
    )
    dma = pltpu.SemaphoreType.DMA
    fields = [field] * 8 + [rows] * 2
    out = pl.pallas_call(
        functools.partial(kernel, n_space),
        out_shape=pltpu.VMEM((3, NV, 8, 128), f32),
        in_specs=[hbm] * 9,
        out_specs=vmem,
        scratch_shapes=[state, state, field_i, field_i, field, pltpu.VMEM((2, NV, 8, 128), f32)]
        + [pltpu.SMEM((LEVELS,), f32), pltpu.SMEM((4, 8), i32), pltpu.SMEM((1,), i32), pltpu.SMEM((2 * STEPS,), f32)]
        + fields
        + fields
        + [edge] * 4
        + [pltpu.VMEM((3, 8, 128), i32)] * 4
        + [pltpu.VMEM((2, 2, 3, 8, 8, 128), f32)]
        + [pltpu.VMEM((2, 3, 8, 8, 128), f32)] * 2
        + [pltpu.VMEM((4, 2, 3, 2, 8, 128), f32)] * 2
        + [pltpu.VMEM((2, 3, 8, 8, 128), f32)] * 2
        + [dma((9,)), dma((8,)), dma((8,)), dma((8,)), dma((8,)), dma((4,)), dma((2, FIXED)), dma((2, FIXED))]
        + [dma((2,))] * 2
        + [dma((4, 2))] * 4
        + [dma((2,))] * 2,
        compiler_params=pltpu.CompilerParams(
            collective_id=0, has_side_effects=True, vmem_limit_bytes=int(60 * 1024 * 1024)
        ),
    )(
        by_vreg(start_states)[0],
        by_vreg(coarse_gain),
        by_vreg(depth_level),
        by_vreg(wet),
        by_vreg(coriolis),
        by_vreg(tide),
        depth_table,
        neighbour.T,
        block_count,
    )
    return jnp.swapaxes(out, 1, 2).reshape(1, 3, 8, NV * 128)


def solution(mesh):
    return jax.shard_map(
        functools.partial(body, mesh.shape["space"]),
        mesh=mesh,
        in_specs=(
            P("tm", None, "space", None),
            P(None, "space", None),
            P("space", None),
            P(),
            P("space", None),
            P("space"),
            P("space", None),
            P("space", None),
            P(None, "space", None),
        ),
        out_specs=P("tm", None, "space", None),
        check_vma=False,
    )
```

time: 51.8 us -> 44.2 us (0.85)
  local copies, waits for them, and re-layouts: 7.74 us -> 0.75 us
    unnamed x20 -> x1, local copies, waits for them, and re-layouts: 7.74 us -> 0.75 us
where the time goes in v2:
time: 44.2 us; the launch traced here: 44 us
  Pallas kernels  42.6 us (96%)
  local copies, waits for them, and re-layouts  0.75 us (2%)
  between operations  0.66 us (1%)
    pallas_call x1, Pallas kernels, body(): pl.pallas_call(functools.partial(kernel, n_space), out_shape=pltpu.VMEM((...  42.6 us

profile of v2, /device:TPU:1, one launch (start us, length us, event | category | flops | bytes accessed | tf_op | source)
XLA Modules:
  0.0 44.0 jit_solution(18272911358332788312)
XLA Ops:
  0.7 42.6 %shard_map.91 = f32[3,32,8,128]{3,2,1,0:T(8,128)S(1)} custom-call(f32[3,32,8,128]{3,2,1,0:T(8,128)} %bitcast.25, f32[3,32,8,128]{3,2,1,0:T(8,128)} %bitcast.26, s32[32,8,128]{2,1,0:T(8,128)} %bitcast.28, s32[32,8,128]{2,1,0:T(8,128)} %bitcast.29, f32[32,8,128]{2,1,0:T(8,128)} %bitcast.30, f32[2,32,8,128]{3,2,1,0:T(8,128)} %bitcast.27, f32[64]{0:T(128)} %table_hbm.1, ...), custom_call_target="tpu_custom_call" | custom-call | tf_op jit(solution)/shard_map/pallas_call | solution.py:399
  43.3 0.7 %copy.11 = f32[1,3,8,4096]{3,2,1,0:T(8,128)} copy(f32[1,3,8,4096]{3,2,1,0:T(8,128)S(1)} %bitcast.24) | data formatting | bytes 786432

commit v3 on v2

--- a/solution.py
+++ b/solution.py
@@ -13,6 +13,7 @@
 LEVELS = 64
 NV = 32
 FIXED = 5
+SUB = 2
 CHUNK = 16
 MESH = pl.DeviceIdType.MESH
 
@@ -37,10 +38,10 @@
     start_hbm, gain_hbm, level_hbm, wet_hbm, cor_hbm, tide_hbm, table_hbm, nb_hbm, count_hbm,
     out_ref,
     start, gain, lev, wet, cor, tide, table, nb, count, trig,
-    depth_o, mask_o, t0_o, t1_o, c_o, eta_o, u_o, v_o, rf_o, re_o,
-    depth_s, mask_s, t0_s, t1_s, c_s, eta_s, u_s, v_s, rf_s, re_s,
+    depth_o, mask_o, t0_o, t1_o, c_o, u_o, v_o, eta_o, rf_o,
+    depth_s, mask_s, t0_s, t1_s, c_s, u_s, v_s, eta_s, rf_s,
     pack_r, pack_l, got_r, got_l, nb_r, nb_l, nbgot_r, nbgot_l,
-    eo, swap, cpart, cgot, xpart, xgot, final,
+    first_state, factor, eo, swap, cpart, cgot, xpart, xgot, final,
     load_sem, hs_r, hr_r, hs_l, hr_l, nsem, os, orr, ss, sr, cs, cr, xs, xr, fs, fr,
 ):
     m = lax.axis_index("tm")
@@ -126,10 +127,18 @@
         for copy in halos[j]:
             copy.start()
 
-    def fixed(j, into, value_of):
+    def split_rows(a, b):
+        rows = []
+        for j in range(a.shape[0]):
+            rows += [jnp.where(low, a[j], turn(b[j], 64)), jnp.where(low, turn(a[j], 64), b[j])]
+        return jnp.stack(rows)
+
+    def fixed(j, into, value_of, masked=False):
         for half in (core, 1 - core):
-            ks = pl.ds(half * CHUNK, CHUNK)
-            value = value_of(ks)
+            ks, at = pl.ds(half * CHUNK, CHUNK), pl.ds(half * 8, 8)
+            value = split_rows(value_of(0, at), value_of(1, at))
+            if masked:
+                value = (2.0 * mask_o[ks]) * value
             into[ks] = value
             if half is core:
                 packed(value, j, 4 * core)
@@ -138,21 +147,21 @@
                 for copy in halos[j]:
                     copy.start()
 
-    def depth_of(ks):
-        index = lev[ks]
+    def depth_of(i, at):
+        index = lev[i, at]
         return jnp.stack(
-            [jnp.take_along_axis(entries, index[i], axis=1, mode="promise_in_bounds") for i in range(CHUNK)]
+            [jnp.take_along_axis(entries, index[n], axis=1, mode="promise_in_bounds") for n in range(8)]
         )
 
     loads[3].wait()
-    fixed(0, c_o, lambda ks: 0.3 * cor[ks])
+    fixed(0, c_o, lambda i, at: 0.3 * cor[i, at])
     loads[6].wait()
     slot_live = slot < count[0]
     loads[0].wait()
-    fixed(1, mask_o, lambda ks: jnp.where(jnp.logical_and(wet[ks] != 0, slot_live[None]), 0.15, 0.0))
+    fixed(1, mask_o, lambda i, at: jnp.where(jnp.logical_and(wet[i, at] != 0, slot_live[None]), 0.15, 0.0))
     loads[4].wait()
-    fixed(2, t0_o, lambda ks: (2.0 * mask_o[ks]) * tide[0, ks])
-    fixed(3, t1_o, lambda ks: (2.0 * mask_o[ks]) * tide[1, ks])
+    fixed(2, t0_o, lambda i, at: tide[0, i, at], True)
+    fixed(3, t1_o, lambda i, at: tide[1, i, at], True)
     loads[1].wait()
     loads[8].wait()
     entries = jnp.full((8, 128), table[0])
@@ -160,12 +169,12 @@
         entries = jnp.where(lane == n, table[n], entries)
     fixed(4, depth_o, depth_of)
     loads[2].wait()
-    for j, (field, state) in enumerate(((1, u_o), (2, v_o), (0, eta_o))):
+    for j, (field, state, skip) in enumerate(((1, u_o, 0), (2, v_o, 0), (0, eta_o, 1))):
         for k0 in chunks:
-            ks = pl.ds(k0, CHUNK)
-            value = jnp.where(mask_o[ks] > 0.0, start[field, ks], 0.0)
-            start[field, ks] = value
-            state[ks] = value
+            ks, at = pl.ds(k0, CHUNK), pl.ds(k0 // 2, 8)
+            value = jnp.where(mask_o[ks] > 0.0, split_rows(start[field, 0, at], start[field, 1, at]), 0.0)
+            first_state[field, ks] = value
+            state[pl.ds(k0 + skip, CHUNK)] = value
             packed(value, FIXED + j, k0 // 4)
         for copy in halos[FIXED + j]:
             copy.start()
@@ -189,6 +198,10 @@
                 value = jnp.where(m == n, jnp.float32(wave((n * STEPS + j) * (2.0 * math.pi / (SLICES * STEPS)))), value)
             trig[at + j] = value
     loads[5].wait()
+    for field in range(3):
+        for k0 in chunks:
+            at = pl.ds(k0 // 2, 8)
+            factor[field, pl.ds(k0, CHUNK)] = split_rows(gain[field, 0, at], gain[field, 1, at])
 
     onwards = [onward(j) for j in range(FIXED)]
     for j in range(FIXED):
@@ -202,7 +215,7 @@
             from_l, from_r = got_r[j, q], got_l[j, q]
             for i in range(4):
                 both = jnp.where(group == i, from_r, from_l)
-                into[4 * q + i] = turn(both, 64 - 16 * i)
+                into[4 * q + i + (into is eta_s)] = turn(both, 64 - 16 * i)
 
     for copy in n_copies:
         copy.wait_recv()
@@ -229,57 +242,55 @@
         d_strip = turn(jnp.where(first, own_at, strip), -1) - turn(jnp.where(last, own_at, strip), 1)
         return d_own, d_strip
 
-    def slope_y(rows, k0, size, swapped):
-        step = rows[pl.ds(k0 + 1, size + 1)] - rows[pl.ds(k0, size + 1)]
-        here, after = step[:size], step[1:]
-        return jnp.where(low, after, here) if swapped else jnp.where(low, here, after)
-
-    def ends(rows, swapped):
-        if swapped:
-            edge = permuted(jnp.where(low, rows[1], rows[NV]), *y_strip)
+    def slope_y(rows, k0, size):
+        return rows[pl.ds(k0 + 2, size)] - rows[pl.ds(k0, size)]
+
+    def ends(rows, strip):
+        above, below = turn(rows[1], 64), turn(rows[NV], 64)
+        if strip:
+            rows[NV + 1] = jnp.where(low, permuted(above, *y_strip), above)
+            rows[0] = jnp.where(low, below, permuted(below, *y_strip))
         else:
-            edge = permuted(jnp.where(low, rows[NV], rows[1]), *y_own)
-        rows[0] = edge
-        rows[NV + 1] = edge
+            rows[NV + 1] = jnp.where(low, above, permuted(above, *y_own))
+            rows[0] = jnp.where(low, permuted(below, *y_own), below)
 
     for k0 in chunks:
         ks, up = pl.ds(k0, CHUNK), pl.ds(k0 + 1, CHUNK)
-        rf_o[up] = turn(depth_o[ks] * v_o[ks], 64)
-        rf_s[up] = turn(depth_s[ks] * v_s[ks], 64)
+        rf_o[up] = depth_o[ks] * v_o[ks]
+        rf_s[up] = depth_s[ks] * v_s[ks]
     ends(rf_o, False)
     ends(rf_s, True)
 
     def surface(step, more):
         cosine, sine = trig[step], trig[STEPS + step]
-        for k0 in chunks:
-            ks, up = pl.ds(k0, CHUNK), pl.ds(k0 + 1, CHUNK)
+        for k0 in range(0, NV, SUB):
+            ks, up = pl.ds(k0, SUB), pl.ds(k0 + 1, SUB)
             dx_o, dx_s = slope_x(depth_o[ks] * u_o[ks], depth_s[ks] * u_s[ks])
-            for eta, mask, t0, t1, dx, dy, rows, turned in (
-                (eta_o, mask_o, t0_o, t1_o, dx_o, slope_y(rf_o, k0, CHUNK, False), re_o, True),
-                (eta_s, mask_s, t0_s, t1_s, dx_s, slope_y(rf_s, k0, CHUNK, True), re_s, more),
+            for eta, mask, t0, t1, dx, rows in (
+                (eta_o, mask_o, t0_o, t1_o, dx_o, rf_o),
+                (eta_s, mask_s, t0_s, t1_s, dx_s, rf_s),
             ):
-                value = eta[ks] + (t0[ks] * cosine + t1[ks] * sine) - mask[ks] * (dx + dy)
-                eta[ks] = value
-                if turned:
-                    rows[up] = turn(value, 64)
-        ends(re_o, False)
+                dy = slope_y(rows, k0, SUB)
+                eta[up] = eta[up] + (t0[ks] * cosine + t1[ks] * sine) - mask[ks] * (dx + dy)
+        ends(eta_o, False)
         if more:
-            ends(re_s, True)
+            ends(eta_s, True)
 
     def one_step(step, carry):
         surface(step, True)
-        for k0 in chunks:
-            ks, up = pl.ds(k0, CHUNK), pl.ds(k0 + 1, CHUNK)
-            dx_o, dx_s = slope_x(eta_o[ks], eta_s[ks])
-            for u_ref, v_ref, mask, cc, depth, dx, dy, rows in (
-                (u_o, v_o, mask_o, c_o, depth_o, dx_o, slope_y(re_o, k0, CHUNK, False), rf_o),
-                (u_s, v_s, mask_s, c_s, depth_s, dx_s, slope_y(re_s, k0, CHUNK, True), rf_s),
+        for k0 in range(0, NV, SUB):
+            ks, up = pl.ds(k0, SUB), pl.ds(k0 + 1, SUB)
+            dx_o, dx_s = slope_x(eta_o[up], eta_s[up])
+            for u_ref, v_ref, mask, cc, depth, dx, eta, rows in (
+                (u_o, v_o, mask_o, c_o, depth_o, dx_o, eta_o, rf_o),
+                (u_s, v_s, mask_s, c_s, depth_s, dx_s, eta_s, rf_s),
             ):
+                dy = slope_y(eta, k0, SUB)
                 u, v = u_ref[ks], v_ref[ks]
                 u_ref[ks] = 0.985 * u + cc[ks] * v - mask[ks] * dx
                 new_v = 0.985 * v - cc[ks] * u - mask[ks] * dy
                 v_ref[ks] = new_v
-                rows[up] = turn(depth[ks] * new_v, 64)
+                rows[up] = depth[ks] * new_v
         ends(rf_o, False)
         ends(rf_s, True)
         return carry
@@ -292,16 +303,16 @@
 
     def defect(half, s):
         k0 = half * 16 + 8 * s
-        ks = pl.ds(k0, 8)
-        dx, _ = slope_x(eta_o[ks], eta_s[ks], False)
-        dy = slope_y(re_o, k0, 8, False)
+        ks, up = pl.ds(k0, 8), pl.ds(k0 + 1, 8)
+        dx, _ = slope_x(eta_o[up], eta_s[up], False)
+        dy = slope_y(eta_o, k0, 8)
         u, v = u_o[ks], v_o[ks]
         fine = (
-            eta_o[ks],
+            eta_o[up],
             0.985 * u + c_o[ks] * v - mask_o[ks] * dx,
             0.985 * v - c_o[ks] * u - mask_o[ks] * dy,
         )
-        return [fine[f] - gain[f, ks] * start[f, ks] for f in range(3)]
+        return [fine[f] - factor[f, ks] * first_state[f, ks] for f in range(3)]
 
     swaps, c_copies, x_copies, f_copies = {}, {}, {}, []
     for s in range(2):
@@ -320,7 +331,7 @@
 
     for s in range(2):
         swaps[s].wait_recv()
-        cpart[s] = eo[1, s] + gain[:, rows_of(core, s)] * eo[0, s]
+        cpart[s] = eo[1, s] + factor[:, rows_of(core, s)] * eo[0, s]
         for d in (2, 1, 3):
             c_copies[d, s] = pltpu.make_async_remote_copy(
                 cpart.at[s, :, quarter(d)], cgot.at[d, s], cs.at[d, s], cr.at[d, s],
@@ -329,7 +340,7 @@
             c_copies[d, s].start()
 
     for s in range(2):
-        g = gain[:, pl.ds(core * 16 + 8 * s + 2 * chip, 2)]
+        g = factor[:, pl.ds(core * 16 + 8 * s + 2 * chip, 2)]
         g2 = g * g
         g4 = g2 * g2
         inverse = 1.0 / (1.0 - g4 * g4)
@@ -349,19 +360,31 @@
             x_copies[d, s].start()
         xgot[s, :, quarter(0)] = x
 
+    def joined_rows(x):
+        pairs = [(x[2 * j], x[2 * j + 1]) for j in range(x.shape[0] // 2)]
+        return (
+            jnp.stack([jnp.where(low, even, turn(odd, 64)) for even, odd in pairs]),
+            jnp.stack([jnp.where(low, turn(even, 64), odd) for even, odd in pairs]),
+        )
+
     for s in range(2):
         for d in (1, 3, 2):
             x_copies[d, s].wait_recv()
         even = xgot[s]
-        odd = gain[:, rows_of(core, s)] * even + eo[0, s]
-        final[s] = jnp.where(core == 0, odd, even)
-        at = rows_of(core, s)
+        odd = factor[:, rows_of(core, s)] * even + eo[0, s]
+        other, mine = jnp.where(core == 0, odd, even), jnp.where(core == 0, even, odd)
+        for f in range(3):
+            for i, rows in enumerate(joined_rows(other[f])):
+                final[s, f, i] = rows
+        at = pl.ds(core * 8 + 4 * s, 4)
         copy = pltpu.make_async_remote_copy(
-            final.at[s], out_ref.at[:, at], fs.at[s], fr.at[s], device_id=twin, device_id_type=MESH
+            final.at[s], out_ref.at[:, :, at], fs.at[s], fr.at[s], device_id=twin, device_id_type=MESH
         )
         copy.start()
         f_copies.append(copy)
-        out_ref[:, at] = jnp.where(core == 0, even, odd)
+        for f in range(3):
+            for i, rows in enumerate(joined_rows(mine[f])):
+                out_ref[f, i, at] = rows
     for copy in f_copies:
         copy.wait()
 
@@ -380,14 +403,15 @@
 
 def by_vreg(x):
     split = x.reshape(x.shape[:-1] + (NV, 128))
-    return jnp.swapaxes(split, -3, -2)
+    return jnp.swapaxes(split, -3, -2).reshape(x.shape[:-2] + (2, NV // 2, 8, 128))
 
 
 def body(n_space, start_states, coarse_gain, depth_level, depth_table, wet, block_count, neighbour, coriolis, tide):
     f32, i32 = jnp.float32, jnp.int32
     field = pltpu.VMEM((NV, 8, 128), f32)
-    field_i = pltpu.VMEM((NV, 8, 128), i32)
     state = pltpu.VMEM((3, NV, 8, 128), f32)
+    whole = pltpu.VMEM((3, 2, NV // 2, 8, 128), f32)
+    whole_i = pltpu.VMEM((2, NV // 2, 8, 128), i32)
     edge = pltpu.VMEM((8, NV // 4, 8, 128), f32)
     rows = pltpu.VMEM((NV + 2, 8, 128), f32)
     vmem, hbm = (
@@ -395,22 +419,24 @@
         pl.BlockSpec(memory_space=pltpu.HBM),
     )
     dma = pltpu.SemaphoreType.DMA
-    fields = [field] * 8 + [rows] * 2
+    fields = [field] * 7 + [rows] * 2
     out = pl.pallas_call(
         functools.partial(kernel, n_space),
-        out_shape=pltpu.VMEM((3, NV, 8, 128), f32),
+        out_shape=pltpu.VMEM((3, 2, NV // 2, 8, 128), f32),
         in_specs=[hbm] * 9,
         out_specs=vmem,
-        scratch_shapes=[state, state, field_i, field_i, field, pltpu.VMEM((2, NV, 8, 128), f32)]
+        scratch_shapes=[whole, whole, whole_i, whole_i]
+        + [pltpu.VMEM((2, NV // 2, 8, 128), f32), pltpu.VMEM((2, 2, NV // 2, 8, 128), f32)]
         + [pltpu.SMEM((LEVELS,), f32), pltpu.SMEM((4, 8), i32), pltpu.SMEM((1,), i32), pltpu.SMEM((2 * STEPS,), f32)]
         + fields
         + fields
         + [edge] * 4
         + [pltpu.VMEM((3, 8, 128), i32)] * 4
+        + [state, state]
         + [pltpu.VMEM((2, 2, 3, 8, 8, 128), f32)]
         + [pltpu.VMEM((2, 3, 8, 8, 128), f32)] * 2
         + [pltpu.VMEM((4, 2, 3, 2, 8, 128), f32)] * 2
-        + [pltpu.VMEM((2, 3, 8, 8, 128), f32)] * 2
+        + [pltpu.VMEM((2, 3, 8, 8, 128), f32), pltpu.VMEM((2, 3, 2, 4, 8, 128), f32)]
         + [dma((9,)), dma((8,)), dma((8,)), dma((8,)), dma((8,)), dma((4,)), dma((2, FIXED)), dma((2, FIXED))]
         + [dma((2,))] * 2
         + [dma((4, 2))] * 4
@@ -429,7 +455,7 @@
         neighbour.T,
         block_count,
     )
-    return jnp.swapaxes(out, 1, 2).reshape(1, 3, 8, NV * 128)
+    return jnp.swapaxes(out.reshape(3, NV, 8, 128), 1, 2).reshape(1, 3, 8, NV * 128)
 
 
 def solution(mesh):

time: 44.2 us -> 43.9 us (level)
  no operation moved by 1% of the time
where the time goes in v3:
time: 43.9 us; the launch traced here: 43.8 us
  Pallas kernels  42.4 us (97%)
  local copies, waits for them, and re-layouts  0.75 us (2%)
  between operations  0.66 us (2%)
    pallas_call x1, Pallas kernels, body(): pl.pallas_call(functools.partial(kernel, n_space), out_shape=pltpu.VMEM((...  42.4 us

profile of v3, /device:TPU:1, one launch (start us, length us, event | category | flops | bytes accessed | tf_op | source)
XLA Modules:
  0.0 43.8 jit_solution(12216655915957943071)
XLA Ops:
  0.7 42.4 %shard_map.91 = f32[3,2,16,8,128]{4,3,2,1,0:T(8,128)S(1)} custom-call(f32[3,2,16,8,128]{4,3,2,1,0:T(8,128)} %bitcast.37, f32[3,2,16,8,128]{4,3,2,1,0:T(8,128)} %bitcast.38, s32[2,16,8,128]{3,2,1,0:T(8,128)} %bitcast.40, s32[2,16,8,128]{3,2,1,0:T(8,128)} %bitcast.41, f32[2,16,8,128]{3,2,1,0:T(8,128)} %bitcast.42, f32[2,2,16,8,128]{4,3,2,1,0:T(8,128)} %bitcast.39, ...), custom_call_target="tpu_custom_call" | custom-call | tf_op jit(solution)/shard_map/pallas_call | solution.py:423
  43.1 0.7 %copy.11 = f32[1,3,8,4096]{3,2,1,0:T(8,128)} copy(f32[1,3,8,4096]{3,2,1,0:T(8,128)S(1)} %bitcast.36) | data formatting | bytes 786432

commit v4 on v3

--- a/solution.py
+++ b/solution.py
@@ -75,7 +75,7 @@
         ]
     ):
         loads.append(pltpu.make_async_copy(src, dst, load_sem.at[j]))
-    for j in (3, 6, 0, 4, 8, 1, 2, 7, 5):
+    for j in (3, 7, 6, 0, 4, 8, 1, 2, 5):
         loads[j].start()
 
     lane = lanes()
@@ -155,6 +155,19 @@
 
     loads[3].wait()
     fixed(0, c_o, lambda i, at: 0.3 * cor[i, at])
+    loads[7].wait()
+    def by_slot(side):
+        entry = jnp.full((8, 128), nb[side, 0])
+        for s in range(1, 8):
+            entry = jnp.where(slot == s, nb[side, s], entry)
+        return entry
+
+    n_own, s_own, e_own, w_own = [by_slot(j) for j in range(4)]
+    for j, (to_right, to_left) in enumerate([(n_own, n_own), (s_own, s_own), (e_own, w_own)]):
+        nb_r[j] = to_right
+        nb_l[j] = to_left
+    for copy in n_copies:
+        copy.start()
     loads[6].wait()
     slot_live = slot < count[0]
     loads[0].wait()
@@ -178,19 +191,6 @@
             packed(value, FIXED + j, k0 // 4)
         for copy in halos[FIXED + j]:
             copy.start()
-    loads[7].wait()
-    def by_slot(side):
-        entry = jnp.full((8, 128), nb[side, 0])
-        for s in range(1, 8):
-            entry = jnp.where(slot == s, nb[side, s], entry)
-        return entry
-
-    n_own, s_own, e_own, w_own = [by_slot(j) for j in range(4)]
-    for j, (to_right, to_left) in enumerate([(n_own, n_own), (s_own, s_own), (e_own, w_own)]):
-        nb_r[j] = to_right
-        nb_l[j] = to_left
-    for copy in n_copies:
-        copy.start()
     for j in range(STEPS):
         for at, wave in ((0, math.cos), (STEPS, math.sin)):
             value = jnp.float32(0.0)

time: 43.9 us -> 43.8 us (level)
  no operation moved by 1% of the time
where the time goes in v4:
time: 43.8 us; the launch traced here: 43.7 us
  Pallas kernels  42.2 us (96%)
  local copies, waits for them, and re-layouts  0.75 us (2%)
  between operations  0.66 us (2%)
    pallas_call x1, Pallas kernels, body(): pl.pallas_call(functools.partial(kernel, n_space), out_shape=pltpu.VMEM((...  42.2 us

profile of v4, /device:TPU:1, one launch (start us, length us, event | category | flops | bytes accessed | tf_op | source)
XLA Modules:
  0.0 43.7 jit_solution(1068172636801796840)
XLA Ops:
  0.7 42.2 %shard_map.91 = f32[3,2,16,8,128]{4,3,2,1,0:T(8,128)S(1)} custom-call(f32[3,2,16,8,128]{4,3,2,1,0:T(8,128)} %bitcast.37, f32[3,2,16,8,128]{4,3,2,1,0:T(8,128)} %bitcast.38, s32[2,16,8,128]{3,2,1,0:T(8,128)} %bitcast.40, s32[2,16,8,128]{3,2,1,0:T(8,128)} %bitcast.41, f32[2,16,8,128]{3,2,1,0:T(8,128)} %bitcast.42, f32[2,2,16,8,128]{4,3,2,1,0:T(8,128)} %bitcast.39, ...), custom_call_target="tpu_custom_call" | custom-call | tf_op jit(solution)/shard_map/pallas_call | solution.py:423
  42.9 0.7 %copy.11 = f32[1,3,8,4096]{3,2,1,0:T(8,128)} copy(f32[1,3,8,4096]{3,2,1,0:T(8,128)S(1)} %bitcast.36) | data formatting | bytes 786432
